TPU v7x, 32 devices: a whole 2x2x4 slice. The times are simulated.
32 devices in a mesh: cfg: 1, pair: 16 (over z, y, x), blk: 2 (over core).
Axes of the slice: x: 2, y: 2, z: 4, core: 2. Of those that a mesh axis runs over, the one named last changes fastest.
Arguments:
- elementals: bfloat16 [16, 8, 2, 65536], P('cfg', None, None, ('pair', 'blk')), may hold values from -0.079589844 to 0.079589844
- perambulator: bfloat16 [16, 2, 1024, 1024], P(('cfg', 'pair'), None, None, 'blk'), may hold values from -0.1875 to 0.1875
- pairs: int32 [16, 2], replicated, may hold values from 0 to 15, as said below
- elem_index: int32 [16, 24], replicated, may hold values from 0 to 7
- coef_code: int32 [16, 24, 4, 4], replicated, may hold values from -2 to 2
- term_count: int32 [16], replicated, may hold values from 12 to 24, as said below
Outputs:
- correlator: float32 [16, 2], P(('cfg', 'pair'))
Inputs may be any that keep to these rules, and one draw needn't show every extreme that they name: `pairs`: pair p + 8 lists the two timeslices of pair p in reverse order; the two timeslices of a pair differ. `term_count`: some pair uses all 24 terms.
All inputs are finite; a program needn't handle non-finite values.
Results may differ from a plain program's by a relative error of at most 0.0057.
Values may be sent and summed in bfloat16 or wider, within the bound.
No kernel may reach another device: no remote copies, remote signals or barrier semaphores. Data moves between devices by JAX's collectives and lax.ppermute only.
A program may use at most 64 MiB of HBM per device.

v0:
```python
import functools

import jax
import jax.numpy as jnp
from jax import lax
from jax.experimental import pallas as pl
from jax.experimental.pallas import tpu as pltpu
from jax.sharding import PartitionSpec as P


F32 = jnp.float32
BF16 = jnp.bfloat16
MIB = 1 << 20

ANY = pl.BlockSpec(memory_space=pl.ANY)
VMEM = pl.BlockSpec(memory_space=pltpu.VMEM)
SMEM = pl.BlockSpec(memory_space=pltpu.SMEM)


def pick_kernel(few, times_ref, table_ref, few_ref, rest_ref, home_ref, left):
    half = home_ref.shape[0]
    side = lax.axis_index("pair") // half
    stores = []
    for n in range(2 * half):
        pair = ((1 - side) * half + n) if n < half else (side * half + n - half)
        out = few_ref.at[n] if n < few else rest_ref.at[n - few] if n < half else home_ref.at[n - half]
        stores.append(pltpu.make_async_copy(table_ref.at[times_ref[0, pair]], out, left.at[n]))
    for store in stores:
        store.start()
    for store in stores:
        store.wait()


def pick(table, times, few, half):
    counts = (few, half - few, half)
    return pl.pallas_call(
        functools.partial(pick_kernel, few),
        out_shape=[jax.ShapeDtypeStruct((n, *table.shape[1:]), table.dtype) for n in counts],
        in_specs=[SMEM, VMEM],
        out_specs=[ANY] * 3,
        scratch_shapes=[pltpu.SemaphoreType.DMA((2 * half,))],
        cost_estimate=pl.CostEstimate(
            flops=0, bytes_accessed=4 * table.size, transcendentals=0
        ),
        name="pick",
    )(times, table)


def sort_kernel(half, rows, nv, prop_ref, out_ref):
    columns = prop_ref.shape[-1]
    wide = columns // nv
    quarter = nv // 4
    source = lax.broadcasted_iota(jnp.int32, (columns, columns), 0)
    target = lax.broadcasted_iota(jnp.int32, (columns, columns), 1)
    place = lax.rem(target, quarter)
    b = lax.rem(target // quarter, wide)
    side = lax.rem(target // (quarter * wide), 2)
    core = target // (2 * quarter * wide)
    device = side * half + place // rows
    wanted = b * nv + (device * 2 + core) * rows + lax.rem(place, rows)
    order = jnp.where(source == wanted, 1.0, 0.0).astype(BF16)
    width = out_ref.shape[-1]
    for c in range(2):
        sorted_part = jnp.dot(prop_ref[c], order, preferred_element_type=F32).astype(BF16)
        for tile in range(4):
            out_ref[tile, c] = sorted_part[:, tile * width : (tile + 1) * width]


def sort(half, rows, nv, prop):
    _, order, columns = prop.shape
    return pl.pallas_call(
        functools.partial(sort_kernel, half, rows, nv),
        out_shape=jax.ShapeDtypeStruct((4, 2, order, columns // 4), BF16),
        in_specs=[VMEM],
        out_specs=VMEM,
        compiler_params=pltpu.CompilerParams(vmem_limit_bytes=16 * MIB),
        cost_estimate=pl.CostEstimate(
            flops=4 * order * columns**2, bytes_accessed=8 * order * columns, transcendentals=0
        ),
        name="sort",
    )(prop)


def combine(ns, weight_ref, elem_ref, phi_ref):
    nop, _, rows, nv = elem_ref.shape
    span = weight_ref.shape[1] // nop
    shape = (span, nop * span)
    unit = lax.rem(lax.broadcasted_iota(jnp.int32, shape, 1), span) == lax.broadcasted_iota(jnp.int32, shape, 0)
    spread = jnp.concatenate(
        [jnp.where(unit, weight_ref[n : n + 1, :], 0.0).astype(BF16) for n in range(ns * ns)], axis=0
    )
    for c in range(2):
        for first in range(0, rows, span):
            parts = jnp.concatenate([elem_ref[o, c, first : first + span, :] for o in range(nop)], axis=0)
            total = jnp.dot(spread, parts, preferred_element_type=F32).astype(BF16)
            for n in range(ns * ns):
                row = n // ns * rows + first
                phi_ref[c, row : row + span, n % ns * nv : (n % ns + 1) * nv] = total[n * span : (n + 1) * span]


def tiles_of(stage):
    core = lax.axis_index("blk")
    side = lax.axis_index("pair") // (lax.axis_size("pair") // 2)
    swap = core ^ side
    if stage == "early":
        return (side, core), (side, 1 - core), (1 - side, swap), (1 - side, 1 - swap)
    return (side, swap), (side, 1 - swap), (1 - side, core), (1 - side, 1 - core)


def dress_kernel(ns, stage, *refs):
    weight_ref, elem_ref, own_ref, other_ref, *outs, phi = refs[:-2]
    held, arrived = refs[-2:]
    core = lax.axis_index("blk")
    loads = []
    for n, (s, c) in enumerate(tiles_of(stage)):
        pair = [
            pltpu.make_async_copy(ref.at[c * 2 + s], held.at[n, place], arrived.at[n, m])
            for m, (ref, place) in enumerate(((own_ref, core), (other_ref, 1 - core)))
        ]
        for load in pair:
            load.start()
        loads.append(pair)
    combine(ns, weight_ref, elem_ref, phi)
    width = held.shape[-1]
    dot = functools.partial(jnp.dot, preferred_element_type=F32)
    for n, out in enumerate(outs):
        for load in loads[n]:
            load.wait()
        prop_real, prop_imag = (
            jnp.concatenate([held[n, 0, c], held[n, 1, c]], axis=1) for c in range(2)
        )
        real = dot(phi[0], prop_real) - dot(phi[1], prop_imag)
        imag = dot(phi[0], prop_imag) + dot(phi[1], prop_real)
        for place in range(2):
            part = slice(place * width, (place + 1) * width)
            out[place, 0] = real[:, part].astype(BF16)
            out[place, 1] = imag[:, part].astype(BF16)


def dress(stage, weight, elem, own, other, ns):
    order, width = own.shape[2:]
    rows = ns * elem.shape[2]
    block = jax.ShapeDtypeStruct((2, 2, rows, width), BF16)
    return pl.pallas_call(
        functools.partial(dress_kernel, ns, stage),
        out_shape=[block] * 4,
        in_specs=[VMEM, VMEM, ANY, ANY],
        out_specs=[VMEM] * 4,
        scratch_shapes=[
            pltpu.VMEM((2, rows, order), BF16),
            pltpu.VMEM((4, 2, *own.shape[1:]), BF16),
            pltpu.SemaphoreType.DMA((4, 2)),
        ],
        cost_estimate=pl.CostEstimate(
            flops=64 * rows * order * width,
            bytes_accessed=32 * order * width,
            transcendentals=0,
        ),
        compiler_params=pltpu.CompilerParams(vmem_limit_bytes=16 * MIB),
    )(weight, elem, own, other)


def trace_kernel(mine_ref, theirs_ref, before_ref, out_ref):
    width = mine_ref.shape[-1]
    real = imag = None
    for block in range(2):
        span = slice(block * width, (block + 1) * width)
        left = [
            jnp.concatenate([mine_ref[0, c, span, :], mine_ref[1, c, span, :]], axis=1)
            for c in range(2)
        ]
        right = [theirs_ref[block, c] for c in range(2)]
        dot = functools.partial(jnp.dot, preferred_element_type=F32)
        re = dot(left[0], right[0]) - dot(left[1], right[1])
        im = dot(left[0], right[1]) + dot(left[1], right[0])
        real = re if real is None else real + re
        imag = im if imag is None else imag + im
    shape = real.shape
    diagonal = lax.broadcasted_iota(jnp.int32, shape, 0) == lax.broadcasted_iota(jnp.int32, shape, 1)
    real = jnp.sum(jnp.where(diagonal, real, 0.0))
    imag = jnp.sum(jnp.where(diagonal, imag, 0.0))
    lane = lax.broadcasted_iota(jnp.int32, out_ref.shape, 1)
    out_ref[...] = before_ref[...] + jnp.where(lane == 0, real, jnp.where(lane == 1, imag, 0.0))


def trace(mine, theirs, before):
    return pl.pallas_call(
        trace_kernel,
        out_shape=jax.ShapeDtypeStruct(before.shape, F32),
        in_specs=[VMEM] * 3,
        out_specs=VMEM,
        cost_estimate=pl.CostEstimate(
            flops=8 * mine.shape[2] ** 3, bytes_accessed=4 * mine.size, transcendentals=0
        ),
        compiler_params=pltpu.CompilerParams(vmem_limit_bytes=4 * MIB),
        name="trace",
    )(mine, theirs, before)


def shards(elementals, perambulator, pairs, elem_index, coef_code, term_count):
    peers = lax.axis_size("pair")
    half = peers // 2
    me = lax.axis_index("pair")
    nop, entries = elementals.shape[1], elementals.shape[-1]
    nterms, ns = elem_index.shape[1], coef_code.shape[-1]
    order, _ = perambulator.shape[2:]
    nv = order // ns
    rows = entries // nv

    def across(value, turn):
        moves = []
        for p in range(peers):
            for c in range(2):
                moves.append((p * 2 + c, (p + half) % peers * 2 + (c ^ turn[p // half])))
        return lax.ppermute(value, ("pair", "blk"), moves)

    def beside(value):
        return lax.ppermute(value, "blk", [(0, 1), (1, 0)])

    def within(value):
        groups = [list(range(half)), list(range(half, peers))]
        return lax.all_to_all(value, "pair", 0, 0, axis_index_groups=groups, tiled=True)

    def rows_of(received):
        shaped = received.reshape(half, nop, 2, rows, nv)
        return shaped.transpose(1, 2, 0, 3, 4).reshape(nop, 2, half * rows, nv)

    times = pairs.T
    few = max(half // 4, 1)
    away_few, away_rest, home = pick(elementals, times, few, half)
    crossed_few = across(away_few, (0, 0))
    home = within(home)
    crossed_rest = across(away_rest, (0, 0))

    own = sort(half, rows, nv, perambulator[0])
    other = beside(own)

    used = jnp.arange(nterms) < term_count[me]
    weights = jnp.where(used[:, None, None], coef_code[me], 0)
    named = elem_index[me][None, :] == jnp.arange(nop)[:, None]
    weight = jnp.sum(jnp.where(named[:, :, None, None], weights[None], 0), axis=1)
    weight = (weight.astype(F32) * 0.5).reshape(nop, ns * ns).T
    weight = jnp.repeat(weight, nv // nop, axis=1)

    near, near_turned, mixed, mixed_kept = dress("early", weight, rows_of(home), own, other, ns)
    got_near = across(near, (0, 0))
    got_near_turned = across(near_turned, (1, 1))
    crossed = jnp.concatenate([crossed_few, crossed_rest])
    away = within(crossed)
    got_mixed = across(mixed, (0, 1))

    last, last_kept, far, far_turned = dress("late", weight, rows_of(away), own, other, ns)
    got_last = across(last, (0, 1))

    total = jnp.zeros((1, 2), F32)
    total = trace(far, got_near, total)
    total = trace(far_turned, got_near_turned, total)
    total = trace(mixed_kept, got_mixed, total)
    total = trace(last_kept, got_last, total)

    total += across(total, (0, 0))
    return total + beside(total)


def solution(mesh):
    return jax.shard_map(
        shards,
        mesh=mesh,
        in_specs=(
            P("cfg", None, None, ("pair", "blk")),
            P(("cfg", "pair"), None, None, "blk"),
            P(),
            P(),
            P(),
            P(),
        ),
        out_specs=P(("cfg", "pair"), None),
        check_vma=False,
    )
```

profile of v0, /device:TPU:27, one launch (start us, length us, event | category | flops | bytes accessed | tf_op | source)
XLA Modules:
  0.0 111.9 jit_solution(2738765868065788581)
XLA Ops:
  0.0 0.0 copy-start
  0.0 0.0 copy-start.1
  0.0 1.6 %copy-done.1 = bf16[1,2,1024,512]{3,2,1,0:T(8,128)(2,1)S(1)} copy-done((bf16[1,2,1024,512]{3,2,1,0:T(8,128)(2,1)S(1)}, bf16[1,2,1024,512]{3,2,1,0:T(8,128)(2,1)}, u32[]{:S(2)}) %copy-start.1) | copy-done | bytes 2097176
  1.6 1.3 %sort.1.refs_2_ = bf16[4,2,1024,128]{3,2,1,0:T(8,128)(2,1)S(1)} custom-call(bf16[2,1024,512]{2,1,0:T(8,128)(2,1)S(1)} %bitcast.20), custom_call_target="tpu_custom_call" | custom-call | flops 1073741824 | bytes 4194304 | tf_op jit(solution)/shard_map/sort/pallas_call | solution.py:71
  2.9 0.0 copy-start.2
  2.9 0.7 collective-permute-start.2
  3.7 2.4 %pick.1 = (bf16[2,8,2,2048]{3,2,1,0:T(2,128)(2,1)}, bf16[6,8,2,2048]{3,2,1,0:T(2,128)(2,1)}, bf16[8,8,2,2048]{3,2,1,0:T(2,128)(2,1)}) custom-call(s32[2,16]{1,0:T(2,128)} %bitcast.24, bf16[16,8,2,2048]{3,2,1,0:T(2,128)(2,1)} %table_ref.1), custom_call_target="tpu_custom_call" | custom-call | bytes 2097152 | tf_op jit(solution)/shard_map/pick/pallas_call | solution.py:36
  6.1 4.6 %all-to-all-start.1 = ((bf16[8,8,2,2048]{3,2,1,0:T(2,128)(2,1)}), bf16[8,8,2,2048]{3,2,1,0:T(2,128)(2,1)S(1)}, u32[]{:S(2)}, u32[]{:S(2)}) async-start(bf16[8,8,2,2048]{3,2,1,0:T(2,128)(2,1)} %get-tuple-element.20), calls=%async_computation.1 | async-start | bytes 1048576 | tf_op jit(solution)/shard_map/all_to_all | solution.py:222
  10.7 0.1 collective-permute-start.1
  10.7 2.3 %collective-permute-start = (bf16[2,8,2,2048]{3,2,1,0:T(2,128)(2,1)}, bf16[2,8,2,2048]{3,2,1,0:T(2,128)(2,1)S(1)}, u32[]{:S(2)}, u32[]{:S(2)}) collective-permute-start(bf16[2,8,2,2048]{3,2,1,0:T(2,128)(2,1)} %get-tuple-element.16), channel_id=1, source_target_pairs={{0,16},{1,17},{2,18},{3,19},{4,20},{5,21},{6,22},{7,23},{8,24},{9,... | collective-permute-start | bytes 393224 | tf_op jit(solution)/shard_map/ppermute | solution.py:215
  13.0 0.0 copy-done.2
  13.0 0.6 dynamic_slice.10
  13.6 22.4 %collective-permute-done = bf16[2,8,2,2048]{3,2,1,0:T(2,128)(2,1)S(1)} collective-permute-done((bf16[2,8,2,2048]{3,2,1,0:T(2,128)(2,1)}, bf16[2,8,2,2048]{3,2,1,0:T(2,128)(2,1)S(1)}, u32[]{:S(2)}, u32[]{:S(2)}) %collective-permute-start) | collective-permute-done | bytes 131104 | tf_op jit(solution)/shard_map/ppermute | solution.py:215
  36.0 0.0 collective-permute-done.1
  36.0 1.5 %pad_maximum_fusion = bf16[8,8,2,2048]{3,2,1,0:T(2,128)(2,1)} fusion(bf16[6,8,2,2048]{3,2,1,0:T(2,128)(2,1)S(1)} %collective-permute-done.1, bf16[2,8,2,2048]{3,2,1,0:T(2,128)(2,1)S(1)} %collective-permute-done), kind=kLoop, calls=%fused_computation | loop fusion | flops 262144 | bytes 1048576 | tf_op jit(solution)/shard_map/concatenate | solution.py:248
  37.5 0.0 all-to-all-done.1
  37.5 4.5 %all-to-all-start = ((bf16[8,8,2,2048]{3,2,1,0:T(2,128)(2,1)}), bf16[8,8,2,2048]{3,2,1,0:T(2,128)(2,1)S(1)}, u32[]{:S(2)}, u32[]{:S(2)}) async-start(bf16[8,8,2,2048]{3,2,1,0:T(2,128)(2,1)} %pad_maximum_fusion), calls=%async_computation | async-start | bytes 1048576 | tf_op jit(solution)/shard_map/all_to_all | solution.py:222
  42.1 0.6 iota_compare_fusion.1
  42.7 0.0 copy-done
  42.8 0.7 select_bitcast_fusion
  43.5 0.4 select_reduce_fusion
  43.8 0.1 broadcast_in_dim.47
  43.9 0.1 reshape.44.refs_0_
  44.0 1.2 %reshape.47 = bf16[8,8,2,8,256]{4,3,2,1,0:T(8,128)(2,1)} reshape(bf16[8,8,2,2048]{3,2,1,0:T(2,128)(2,1)S(1)} %all-to-all-done.1) | data formatting | bytes 1048576 | tf_op jit(solution)/shard_map/reshape | solution.py:225
  45.2 1.1 copy.14
  46.3 4.0 %all-to-all-done = bf16[8,8,2,2048]{3,2,1,0:T(2,128)(2,1)S(1)} async-done(((bf16[8,8,2,2048]{3,2,1,0:T(2,128)(2,1)}), bf16[8,8,2,2048]{3,2,1,0:T(2,128)(2,1)S(1)}, u32[]{:S(2)}, u32[]{:S(2)}) %all-to-all-start) | async-done | bytes 524320 | tf_op jit(solution)/shard_map/all_to_all | solution.py:222
  50.2 1.2 %reshape.45 = bf16[8,8,2,8,256]{4,3,2,1,0:T(8,128)(2,1)} reshape(bf16[8,8,2,2048]{3,2,1,0:T(2,128)(2,1)S(1)} %all-to-all-done) | data formatting | bytes 1048576 | tf_op jit(solution)/shard_map/reshape | solution.py:225
  51.4 1.1 copy.15
  52.5 0.0 collective-permute-done.2.refs_3_
  52.5 4.3 %shard_map.65 = (bf16[2,2,256,128]{3,2,1,0:T(8,128)(2,1)S(1)}, bf16[2,2,256,128]{3,2,1,0:T(8,128)(2,1)S(1)}, bf16[2,2,256,128]{3,2,1,0:T(8,128)(2,1)S(1)}, bf16[2,2,256,128]{3,2,1,0:T(8,128)(2,1)S(1)}) custom-call(f32[16,256]{1,0:T(8,128)S(1)} %reshape.44.refs_0_, bf16[8,2,64,256]{3,2,1,0:T(8,128)(2,1)S(1)} %bitcast.22, ...), custom_call_target="tpu_custom_call" | custom-call | flops 2147483648 | bytes 4194304 | tf_op jit(solution)/shard_map/pallas_call | solution.py:144
  56.8 0.1 collective-permute-start.6
  56.8 3.0 %collective-permute-start.5 = (bf16[2,2,256,128]{3,2,1,0:T(8,128)(2,1)S(1)}, bf16[2,2,256,128]{3,2,1,0:T(8,128)(2,1)S(1)}, u32[]{:S(2)}, u32[]{:S(2)}) collective-permute-start(bf16[2,2,256,128]{3,2,1,0:T(8,128)(2,1)S(1)} %get-tuple-element.24), channel_id=1, source_target_pairs={{0,17},{1,16},{2,19},{3,18},{4,21},{5,20},{6,23},{7,22},{8,25},{9,... | collective-permute-start | bytes 786440 | tf_op jit(solution)/shard_map/ppermute | solution.py:215
  59.8 0.0 collective-permute-start.4
  59.9 4.3 %shard_map.64 = (bf16[2,2,256,128]{3,2,1,0:T(8,128)(2,1)S(1)}, bf16[2,2,256,128]{3,2,1,0:T(8,128)(2,1)S(1)}, bf16[2,2,256,128]{3,2,1,0:T(8,128)(2,1)S(1)}, bf16[2,2,256,128]{3,2,1,0:T(8,128)(2,1)S(1)}) custom-call(f32[16,256]{1,0:T(8,128)S(1)} %reshape.44.refs_0_, bf16[8,2,64,256]{3,2,1,0:T(8,128)(2,1)S(1)} %bitcast.21, ...), custom_call_target="tpu_custom_call" | custom-call | flops 2147483648 | bytes 4194304 | tf_op jit(solution)/shard_map/pallas_call | solution.py:144
  64.1 2.3 %collective-permute-start.3 = (bf16[2,2,256,128]{3,2,1,0:T(8,128)(2,1)S(1)}, bf16[2,2,256,128]{3,2,1,0:T(8,128)(2,1)S(1)}, u32[]{:S(2)}, u32[]{:S(2)}) collective-permute-start(bf16[2,2,256,128]{3,2,1,0:T(8,128)(2,1)S(1)} %get-tuple-element.19), channel_id=1, source_target_pairs={{0,16},{1,17},{2,18},{3,19},{4,20},{5,21},{6,22},{7,23},{8,24},{9,... | collective-permute-start | bytes 786440 | tf_op jit(solution)/shard_map/ppermute | solution.py:215
  66.4 21.8 %collective-permute-done.6.theirs_ref = bf16[2,2,256,128]{3,2,1,0:T(8,128)(2,1)S(1)} collective-permute-done((bf16[2,2,256,128]{3,2,1,0:T(8,128)(2,1)S(1)}, bf16[2,2,256,128]{3,2,1,0:T(8,128)(2,1)S(1)}, u32[]{:S(2)}, u32[]{:S(2)}) %collective-permute-start.6) | collective-permute-done | bytes 262176 | tf_op jit(solution)/shard_map/ppermute | solution.py:215
  88.2 0.4 trace.4.before_ref
  88.6 5.2 %collective-permute-done.5.theirs_ref = bf16[2,2,256,128]{3,2,1,0:T(8,128)(2,1)S(1)} collective-permute-done((bf16[2,2,256,128]{3,2,1,0:T(8,128)(2,1)S(1)}, bf16[2,2,256,128]{3,2,1,0:T(8,128)(2,1)S(1)}, u32[]{:S(2)}, u32[]{:S(2)}) %collective-permute-start.5) | collective-permute-done | bytes 262176 | tf_op jit(solution)/shard_map/ppermute | solution.py:215
  93.8 0.4 trace.5.before_ref
  94.3 5.2 %collective-permute-done.4.theirs_ref = bf16[2,2,256,128]{3,2,1,0:T(8,128)(2,1)S(1)} collective-permute-done((bf16[2,2,256,128]{3,2,1,0:T(8,128)(2,1)S(1)}, bf16[2,2,256,128]{3,2,1,0:T(8,128)(2,1)S(1)}, u32[]{:S(2)}, u32[]{:S(2)}) %collective-permute-start.4) | collective-permute-done | bytes 262176 | tf_op jit(solution)/shard_map/ppermute | solution.py:215
  99.5 0.4 trace.6.before_ref
  99.9 5.2 %collective-permute-done.3.theirs_ref = bf16[2,2,256,128]{3,2,1,0:T(8,128)(2,1)S(1)} collective-permute-done((bf16[2,2,256,128]{3,2,1,0:T(8,128)(2,1)S(1)}, bf16[2,2,256,128]{3,2,1,0:T(8,128)(2,1)S(1)}, u32[]{:S(2)}, u32[]{:S(2)}) %collective-permute-start.3) | collective-permute-done | bytes 262176 | tf_op jit(solution)/shard_map/ppermute | solution.py:215
  105.1 0.4 trace.7
  105.5 0.1 collective-permute-start.7
  105.6 3.3 %collective-permute-done.7 = f32[1,2]{1,0:T(1,128)S(1)} collective-permute-done((f32[1,2]{1,0:T(1,128)S(1)}, f32[1,2]{1,0:T(1,128)S(1)}, u32[]{:S(2)}, u32[]{:S(2)}) %collective-permute-start.7) | collective-permute-done | bytes 40 | tf_op jit(solution)/shard_map/ppermute | solution.py:215
  108.9 1.6 %collective-permute-start.8 = (f32[1,2]{1,0:T(1,128)S(1)}, f32[1,2]{1,0:T(1,128)S(1)}, u32[]{:S(2)}, u32[]{:S(2)}) collective-permute-start(f32[1,2]{1,0:T(1,128)S(1)} %add.12), channel_id=1, source_target_pairs={{0,1},{1,0},{2,3},{3,2},{4,5},{5,4},{6,7},{7,6},{8,9},{9,8},{10,11... | collective-permute-start | bytes 32 | tf_op jit(solution)/shard_map/ppermute | solution.py:218
  110.5 0.8 collective-permute-done.8
  111.3 0.5 add.13
  (5 shorter events, 0.0 us)
Async XLA Ops:
  0.0 42.7 %copy-start = (s32[16,24]{1,0:T(8,128)S(1)}, s32[16,24]{1,0:T(8,128)}, u32[]{:S(2)}) copy-start(s32[16,24]{1,0:T(8,128)} %param.9) | copy-start | bytes 4612
  0.0 1.6 %copy-start.1 = (bf16[1,2,1024,512]{3,2,1,0:T(8,128)(2,1)S(1)}, bf16[1,2,1024,512]{3,2,1,0:T(8,128)(2,1)}, u32[]{:S(2)}) copy-start(bf16[1,2,1024,512]{3,2,1,0:T(8,128)(2,1)} %param.7) | copy-start | bytes 6291460
  2.9 10.1 %copy-start.2 = (s32[16]{0:T(128)S(1)}, s32[16]{0:T(128)}, u32[]{:S(2)}) copy-start(s32[16]{0:T(128)} %param.11) | copy-start | bytes 196
  2.9 49.5 %collective-permute-start.2 = (bf16[4,2,1024,128]{3,2,1,0:T(8,128)(2,1)S(1)}, bf16[4,2,1024,128]{3,2,1,0:T(8,128)(2,1)}, u32[]{:S(2)}, u32[]{:S(2)}) collective-permute-start(bf16[4,2,1024,128]{3,2,1,0:T(8,128)(2,1)S(1)} %sort.1.refs_2_), channel_id=1, source_target_pairs={{0,1},{1,0},{2,3},{3,2},{4,5},{5,4},{6,7},{7,6},{8,9},{9,8},{10,11... | collective-permute-start | bytes 6291464 | tf_op jit(solution)/shard_map/ppermute | solution.py:218
  6.1 31.4 %all-to-all-start.1 = ((bf16[8,8,2,2048]{3,2,1,0:T(2,128)(2,1)}), bf16[8,8,2,2048]{3,2,1,0:T(2,128)(2,1)S(1)}, u32[]{:S(2)}, u32[]{:S(2)}) async-start(bf16[8,8,2,2048]{3,2,1,0:T(2,128)(2,1)} %get-tuple-element.20), calls=%async_computation.1 | async-start | bytes 1048576 | tf_op jit(solution)/shard_map/all_to_all | solution.py:222
  10.7 25.3 %collective-permute-start.1 = (bf16[6,8,2,2048]{3,2,1,0:T(2,128)(2,1)}, bf16[6,8,2,2048]{3,2,1,0:T(2,128)(2,1)S(1)}, u32[]{:S(2)}, u32[]{:S(2)}) collective-permute-start(bf16[6,8,2,2048]{3,2,1,0:T(2,128)(2,1)} %get-tuple-element.17), channel_id=1, source_target_pairs={{0,16},{1,17},{2,18},{3,19},{4,20},{5,21},{6,22},{7,23},{8,24},{9,... | collective-permute-start | bytes 1179656 | tf_op jit(solution)/shard_map/ppermute | solution.py:215
  10.7 25.3 %collective-permute-start = (bf16[2,8,2,2048]{3,2,1,0:T(2,128)(2,1)}, bf16[2,8,2,2048]{3,2,1,0:T(2,128)(2,1)S(1)}, u32[]{:S(2)}, u32[]{:S(2)}) collective-permute-start(bf16[2,8,2,2048]{3,2,1,0:T(2,128)(2,1)} %get-tuple-element.16), channel_id=1, source_target_pairs={{0,16},{1,17},{2,18},{3,19},{4,20},{5,21},{6,22},{7,23},{8,24},{9,... | collective-permute-start | bytes 393224 | tf_op jit(solution)/shard_map/ppermute | solution.py:215
  37.5 12.7 %all-to-all-start = ((bf16[8,8,2,2048]{3,2,1,0:T(2,128)(2,1)}), bf16[8,8,2,2048]{3,2,1,0:T(2,128)(2,1)S(1)}, u32[]{:S(2)}, u32[]{:S(2)}) async-start(bf16[8,8,2,2048]{3,2,1,0:T(2,128)(2,1)} %pad_maximum_fusion), calls=%async_computation | async-start | bytes 1048576 | tf_op jit(solution)/shard_map/all_to_all | solution.py:222
  56.8 31.5 %collective-permute-start.6 = (bf16[2,2,256,128]{3,2,1,0:T(8,128)(2,1)S(1)}, bf16[2,2,256,128]{3,2,1,0:T(8,128)(2,1)S(1)}, u32[]{:S(2)}, u32[]{:S(2)}) collective-permute-start(bf16[2,2,256,128]{3,2,1,0:T(8,128)(2,1)S(1)} %get-tuple-element.26), channel_id=1, source_target_pairs={{0,16},{1,17},{2,18},{3,19},{4,20},{5,21},{6,22},{7,23},{8,24},{9,... | collective-permute-start | bytes 786440 | tf_op jit(solution)/shard_map/ppermute | solution.py:215
  56.8 37.0 %collective-permute-start.5 = (bf16[2,2,256,128]{3,2,1,0:T(8,128)(2,1)S(1)}, bf16[2,2,256,128]{3,2,1,0:T(8,128)(2,1)S(1)}, u32[]{:S(2)}, u32[]{:S(2)}) collective-permute-start(bf16[2,2,256,128]{3,2,1,0:T(8,128)(2,1)S(1)} %get-tuple-element.24), channel_id=1, source_target_pairs={{0,17},{1,16},{2,19},{3,18},{4,21},{5,20},{6,23},{7,22},{8,25},{9,... | collective-permute-start | bytes 786440 | tf_op jit(solution)/shard_map/ppermute | solution.py:215
  59.8 39.6 %collective-permute-start.4 = (bf16[2,2,256,128]{3,2,1,0:T(8,128)(2,1)S(1)}, bf16[2,2,256,128]{3,2,1,0:T(8,128)(2,1)S(1)}, u32[]{:S(2)}, u32[]{:S(2)}) collective-permute-start(bf16[2,2,256,128]{3,2,1,0:T(8,128)(2,1)S(1)} %get-tuple-element.22), channel_id=1, source_target_pairs={{0,16},{1,17},{2,18},{3,19},{4,20},{5,21},{6,22},{7,23},{8,24},{9,... | collective-permute-start | bytes 786440 | tf_op jit(solution)/shard_map/ppermute | solution.py:215
  64.1 40.9 %collective-permute-start.3 = (bf16[2,2,256,128]{3,2,1,0:T(8,128)(2,1)S(1)}, bf16[2,2,256,128]{3,2,1,0:T(8,128)(2,1)S(1)}, u32[]{:S(2)}, u32[]{:S(2)}) collective-permute-start(bf16[2,2,256,128]{3,2,1,0:T(8,128)(2,1)S(1)} %get-tuple-element.19), channel_id=1, source_target_pairs={{0,16},{1,17},{2,18},{3,19},{4,20},{5,21},{6,22},{7,23},{8,24},{9,... | collective-permute-start | bytes 786440 | tf_op jit(solution)/shard_map/ppermute | solution.py:215
  105.5 3.4 %collective-permute-start.7 = (f32[1,2]{1,0:T(1,128)S(1)}, f32[1,2]{1,0:T(1,128)S(1)}, u32[]{:S(2)}, u32[]{:S(2)}) collective-permute-start(f32[1,2]{1,0:T(1,128)S(1)} %trace.7), channel_id=1, source_target_pairs={{0,16},{1,17},{2,18},{3,19},{4,20},{5,21},{6,22},{7,23},{8,24},{9,... | collective-permute-start | bytes 32 | tf_op jit(solution)/shard_map/ppermute | solution.py:215
  108.9 2.5 %collective-permute-start.8 = (f32[1,2]{1,0:T(1,128)S(1)}, f32[1,2]{1,0:T(1,128)S(1)}, u32[]{:S(2)}, u32[]{:S(2)}) collective-permute-start(f32[1,2]{1,0:T(1,128)S(1)} %add.12), channel_id=1, source_target_pairs={{0,1},{1,0},{2,3},{3,2},{4,5},{5,4},{6,7},{7,6},{8,9},{9,8},{10,11... | collective-permute-start | bytes 32 | tf_op jit(solution)/shard_map/ppermute | solution.py:218
where the time goes:
time: 112 us
  waiting for transfers between devices  67.8 us (61%)
  starting transfers between devices  19.4 us (17%)
  Pallas kernels  13.9 us (12%)
  local copies, waits for them, and re-layouts  6.85 us (6%)
  other arithmetic  3.73 us (3%)
    ppermute x7, waiting for transfers between devices, across(): return lax.ppermute(value, ('pair', 'blk'), moves)  63.1 us
    all_to_all x2, starting transfers between devices, within(): lax.all_to_all(value, 'pair', 0, 0, axis_index_groups=groups, tiled=True)  9.15 us
    pallas_call x2, Pallas kernels, dress(): pl.pallas_call(functools.partial(dress_kernel, ns, stage), out_shape=[blo...  8.55 us
    ppermute x7, starting transfers between devices, across(): return lax.ppermute(value, ('pair', 'blk'), moves)  7.84 us
    reshape x4, local copies, waits for them, and re-layouts, rows_of(): shaped = received.reshape(half, nop, 2, rows, nv)  4.47 us
    all_to_all x2, waiting for transfers between devices, within(): lax.all_to_all(value, 'pair', 0, 0, axis_index_groups=groups, tiled=True)  3.96 us
    pallas_call x1, Pallas kernels, pick(): pl.pallas_call(functools.partial(pick_kernel, few), out_shape=[jax.ShapeD...  2.4 us
    ppermute x2, starting transfers between devices, beside(): return lax.ppermute(value, 'blk', [(0, 1), (1, 0)])  2.38 us
  transfers between devices with their start and end apart: 11, of which 8 were waited for; matrix products, arithmetic and copies ran while one was open for 8% of the time, Pallas kernels for 7%

commit v1 on v0

--- a/solution.py
+++ b/solution.py
@@ -17,27 +17,26 @@
 SMEM = pl.BlockSpec(memory_space=pltpu.SMEM)
 
 
-def pick_kernel(few, times_ref, table_ref, few_ref, rest_ref, home_ref, left):
+def pick_kernel(times_ref, table_ref, away_ref, home_ref, left):
     half = home_ref.shape[0]
     side = lax.axis_index("pair") // half
     stores = []
-    for n in range(2 * half):
-        pair = ((1 - side) * half + n) if n < half else (side * half + n - half)
-        out = few_ref.at[n] if n < few else rest_ref.at[n - few] if n < half else home_ref.at[n - half]
-        stores.append(pltpu.make_async_copy(table_ref.at[times_ref[0, pair]], out, left.at[n]))
+    for out, first in ((away_ref, (1 - side) * half), (home_ref, side * half)):
+        for n in range(half):
+            time = times_ref[0, first + n]
+            stores.append(pltpu.make_async_copy(table_ref.at[time], out.at[n], left.at[len(stores)]))
     for store in stores:
         store.start()
     for store in stores:
         store.wait()
 
 
-def pick(table, times, few, half):
-    counts = (few, half - few, half)
-    return pl.pallas_call(
-        functools.partial(pick_kernel, few),
-        out_shape=[jax.ShapeDtypeStruct((n, *table.shape[1:]), table.dtype) for n in counts],
+def pick(table, times, half):
+    return pl.pallas_call(
+        pick_kernel,
+        out_shape=[jax.ShapeDtypeStruct((half, *table.shape[1:]), table.dtype)] * 2,
         in_specs=[SMEM, VMEM],
-        out_specs=[ANY] * 3,
+        out_specs=[ANY] * 2,
         scratch_shapes=[pltpu.SemaphoreType.DMA((2 * half,))],
         cost_estimate=pl.CostEstimate(
             flops=0, bytes_accessed=4 * table.size, transcendentals=0
@@ -73,7 +72,6 @@
         out_shape=jax.ShapeDtypeStruct((4, 2, order, columns // 4), BF16),
         in_specs=[VMEM],
         out_specs=VMEM,
-        compiler_params=pltpu.CompilerParams(vmem_limit_bytes=16 * MIB),
         cost_estimate=pl.CostEstimate(
             flops=4 * order * columns**2, bytes_accessed=8 * order * columns, transcendentals=0
         ),
@@ -226,11 +224,9 @@
         return shaped.transpose(1, 2, 0, 3, 4).reshape(nop, 2, half * rows, nv)
 
     times = pairs.T
-    few = max(half // 4, 1)
-    away_few, away_rest, home = pick(elementals, times, few, half)
-    crossed_few = across(away_few, (0, 0))
+    away, home = pick(elementals, times, half)
+    crossed = across(away, (0, 0))
     home = within(home)
-    crossed_rest = across(away_rest, (0, 0))
 
     own = sort(half, rows, nv, perambulator[0])
     other = beside(own)
@@ -245,7 +241,6 @@
     near, near_turned, mixed, mixed_kept = dress("early", weight, rows_of(home), own, other, ns)
     got_near = across(near, (0, 0))
     got_near_turned = across(near_turned, (1, 1))
-    crossed = jnp.concatenate([crossed_few, crossed_rest])
     away = within(crossed)
     got_mixed = across(mixed, (0, 1))
 
@@ -258,8 +253,9 @@
     total = trace(mixed_kept, got_mixed, total)
     total = trace(last_kept, got_last, total)
 
-    total += across(total, (0, 0))
-    return total + beside(total)
+    other = beside(total)
+    there = across(total, (0, 0))
+    return (total + there) + (other + beside(there))
 
 
 def solution(mesh):

time: 112 us -> 112 us (level)
  Pallas kernels: 13.9 us -> 16.8 us
  waiting for transfers between devices: 67.8 us -> 69.7 us
  starting transfers between devices: 19.4 us -> 17.5 us
  local copies, waits for them, and re-layouts: 6.85 us -> 5.22 us
  other arithmetic: 3.73 us -> 2.24 us
    pallas_call x1, Pallas kernels: 1.3 us -> 4.23 us  [sort(): pl.pallas_call(functools.partial(sort_kernel, half, rows, nv), out_shape=...]
    ppermute x7 -> x6, starting transfers between devices: 7.84 us -> 5.53 us  [across(): return lax.ppermute(value, ('pair', 'blk'), moves)]
    ppermute x7 -> x6, waiting for transfers between devices: 63.1 us -> 64.9 us  [across(): return lax.ppermute(value, ('pair', 'blk'), moves)]
    unnamed x6, local copies, waits for them, and re-layouts: 1.61 us -> 0.01 us
    concatenate x1 -> x0, other arithmetic: 1.49 us -> none  [shards(): crossed = jnp.concatenate([crossed_few, crossed_rest])]
    ppermute x2 -> x3, starting transfers between devices: 2.38 us -> 2.87 us  [beside(): return lax.ppermute(value, 'blk', [(0, 1), (1, 0)])]
  transfers between devices with their start and end apart: 11 -> 11, of which waited for: 8 -> 8; matrix products, arithmetic and copies ran while one was open for 8% -> 6% of each run, Pallas kernels for 7% -> 7%
where the time goes in v1:
time: 112 us
  waiting for transfers between devices  69.7 us (62%)
  starting transfers between devices  17.5 us (16%)
  Pallas kernels  16.8 us (15%)
  local copies, waits for them, and re-layouts  5.22 us (5%)
  other arithmetic  2.24 us (2%)
    ppermute x6, waiting for transfers between devices, across(): return lax.ppermute(value, ('pair', 'blk'), moves)  64.9 us
    all_to_all x2, starting transfers between devices, within(): lax.all_to_all(value, 'pair', 0, 0, axis_index_groups=groups, tiled=True)  9.15 us
    pallas_call x2, Pallas kernels, dress(): pl.pallas_call(functools.partial(dress_kernel, ns, stage), out_shape=[blo...  8.55 us
    ppermute x6, starting transfers between devices, across(): return lax.ppermute(value, ('pair', 'blk'), moves)  5.53 us
    reshape x4, local copies, waits for them, and re-layouts, rows_of(): shaped = received.reshape(half, nop, 2, rows, nv)  4.44 us
    pallas_call x1, Pallas kernels, sort(): pl.pallas_call(functools.partial(sort_kernel, half, rows, nv), out_shape=...  4.23 us
    all_to_all x2, waiting for transfers between devices, within(): lax.all_to_all(value, 'pair', 0, 0, axis_index_groups=groups, tiled=True)  3.96 us
    ppermute x3, starting transfers between devices, beside(): return lax.ppermute(value, 'blk', [(0, 1), (1, 0)])  2.87 us
  transfers between devices with their start and end apart: 11, of which 8 were waited for; matrix products, arithmetic and copies ran while one was open for 6% of the time, Pallas kernels for 7%

profile of v1, /device:TPU:27, one launch (start us, length us, event | category | flops | bytes accessed | tf_op | source)
XLA Modules:
  0.0 111.7 jit_solution(6211612237699321058)
XLA Ops:
  0.0 0.0 copy-start
  0.0 4.2 %sort.1.refs_2_ = bf16[4,2,1024,128]{3,2,1,0:T(8,128)(2,1)} custom-call(bf16[2,1024,512]{2,1,0:T(8,128)(2,1)} %bitcast.22), custom_call_target="tpu_custom_call" | custom-call | flops 1073741824 | bytes 4194304 | tf_op jit(solution)/shard_map/sort/pallas_call | solution.py:70
  4.2 0.0 copy-start.2
  4.2 0.7 collective-permute-start.1
  4.9 2.4 %pick.1 = (bf16[8,8,2,2048]{3,2,1,0:T(2,128)(2,1)}, bf16[8,8,2,2048]{3,2,1,0:T(2,128)(2,1)}) custom-call(s32[2,16]{1,0:T(2,128)} %bitcast.24, bf16[16,8,2,2048]{3,2,1,0:T(2,128)(2,1)} %table_ref.1), custom_call_target="tpu_custom_call" | custom-call | bytes 2097152 | tf_op jit(solution)/shard_map/pick/pallas_call | solution.py:35
  7.3 4.6 %all-to-all-start.1 = ((bf16[8,8,2,2048]{3,2,1,0:T(2,128)(2,1)}), bf16[8,8,2,2048]{3,2,1,0:T(2,128)(2,1)S(1)}, u32[]{:S(2)}, u32[]{:S(2)}) async-start(bf16[8,8,2,2048]{3,2,1,0:T(2,128)(2,1)} %get-tuple-element.18), calls=%async_computation.1 | async-start | bytes 1048576 | tf_op jit(solution)/shard_map/all_to_all | solution.py:220
  11.9 0.1 collective-permute-start
  12.0 0.0 copy-done.2
  12.0 0.6 dynamic_slice.10
  12.6 24.8 %collective-permute-done = bf16[8,8,2,2048]{3,2,1,0:T(2,128)(2,1)} collective-permute-done((bf16[8,8,2,2048]{3,2,1,0:T(2,128)(2,1)}, bf16[8,8,2,2048]{3,2,1,0:T(2,128)(2,1)}, u32[]{:S(2)}, u32[]{:S(2)}) %collective-permute-start) | collective-permute-done | bytes 524320 | tf_op jit(solution)/shard_map/ppermute | solution.py:213
  37.4 0.0 all-to-all-done.1
  37.4 4.5 %all-to-all-start = ((bf16[8,8,2,2048]{3,2,1,0:T(2,128)(2,1)}), bf16[8,8,2,2048]{3,2,1,0:T(2,128)(2,1)S(1)}, u32[]{:S(2)}, u32[]{:S(2)}) async-start(bf16[8,8,2,2048]{3,2,1,0:T(2,128)(2,1)} %collective-permute-done), calls=%async_computation | async-start | bytes 1048576 | tf_op jit(solution)/shard_map/all_to_all | solution.py:220
  41.9 0.6 iota_compare_fusion.1
  42.6 0.0 copy-done
  42.6 0.7 select_bitcast_fusion
  43.3 0.4 select_reduce_fusion
  43.7 0.1 broadcast_in_dim.47
  43.8 0.1 reshape.44.refs_0_
  43.9 0.0 copy-start.1
  43.9 1.1 %reshape.47 = bf16[8,8,2,8,256]{4,3,2,1,0:T(8,128)(2,1)} reshape(bf16[8,8,2,2048]{3,2,1,0:T(2,128)(2,1)S(1)} %all-to-all-done.1) | data formatting | bytes 1048576 | tf_op jit(solution)/shard_map/reshape | solution.py:223
  45.0 1.1 copy.14
  46.1 4.0 %all-to-all-done = bf16[8,8,2,2048]{3,2,1,0:T(2,128)(2,1)S(1)} async-done(((bf16[8,8,2,2048]{3,2,1,0:T(2,128)(2,1)}), bf16[8,8,2,2048]{3,2,1,0:T(2,128)(2,1)S(1)}, u32[]{:S(2)}, u32[]{:S(2)}) %all-to-all-start) | async-done | bytes 524320 | tf_op jit(solution)/shard_map/all_to_all | solution.py:220
  50.1 1.1 %reshape.45 = bf16[8,8,2,8,256]{4,3,2,1,0:T(8,128)(2,1)} reshape(bf16[8,8,2,2048]{3,2,1,0:T(2,128)(2,1)S(1)} %all-to-all-done) | data formatting | bytes 1048576 | tf_op jit(solution)/shard_map/reshape | solution.py:223
  51.2 1.1 copy.15
  52.3 0.0 collective-permute-done.1.refs_3_
  52.3 0.0 copy-done.1
  52.3 4.3 %shard_map.65 = (bf16[2,2,256,128]{3,2,1,0:T(8,128)(2,1)S(1)}, bf16[2,2,256,128]{3,2,1,0:T(8,128)(2,1)S(1)}, bf16[2,2,256,128]{3,2,1,0:T(8,128)(2,1)S(1)}, bf16[2,2,256,128]{3,2,1,0:T(8,128)(2,1)S(1)}) custom-call(f32[16,256]{1,0:T(8,128)S(1)} %reshape.44.refs_0_, bf16[8,2,64,256]{3,2,1,0:T(8,128)(2,1)S(1)} %bitcast.21, ...), custom_call_target="tpu_custom_call" | custom-call | flops 2147483648 | bytes 4194304 | tf_op jit(solution)/shard_map/pallas_call | solution.py:142
  56.6 0.1 collective-permute-start.5
  56.7 3.0 %collective-permute-start.4 = (bf16[2,2,256,128]{3,2,1,0:T(8,128)(2,1)S(1)}, bf16[2,2,256,128]{3,2,1,0:T(8,128)(2,1)S(1)}, u32[]{:S(2)}, u32[]{:S(2)}) collective-permute-start(bf16[2,2,256,128]{3,2,1,0:T(8,128)(2,1)S(1)} %get-tuple-element.22), channel_id=1, source_target_pairs={{0,17},{1,16},{2,19},{3,18},{4,21},{5,20},{6,23},{7,22},{8,25},{9,... | collective-permute-start | bytes 786440 | tf_op jit(solution)/shard_map/ppermute | solution.py:213
  59.7 0.0 collective-permute-start.3
  59.7 4.3 %shard_map.64 = (bf16[2,2,256,128]{3,2,1,0:T(8,128)(2,1)S(1)}, bf16[2,2,256,128]{3,2,1,0:T(8,128)(2,1)S(1)}, bf16[2,2,256,128]{3,2,1,0:T(8,128)(2,1)S(1)}, bf16[2,2,256,128]{3,2,1,0:T(8,128)(2,1)S(1)}) custom-call(f32[16,256]{1,0:T(8,128)S(1)} %reshape.44.refs_0_, bf16[8,2,64,256]{3,2,1,0:T(8,128)(2,1)S(1)} %bitcast.20, ...), custom_call_target="tpu_custom_call" | custom-call | flops 2147483648 | bytes 4194304 | tf_op jit(solution)/shard_map/pallas_call | solution.py:142
  64.0 2.3 %collective-permute-start.2 = (bf16[2,2,256,128]{3,2,1,0:T(8,128)(2,1)S(1)}, bf16[2,2,256,128]{3,2,1,0:T(8,128)(2,1)S(1)}, u32[]{:S(2)}, u32[]{:S(2)}) collective-permute-start(bf16[2,2,256,128]{3,2,1,0:T(8,128)(2,1)S(1)} %get-tuple-element.17), channel_id=1, source_target_pairs={{0,16},{1,17},{2,18},{3,19},{4,20},{5,21},{6,22},{7,23},{8,24},{9,... | collective-permute-start | bytes 786440 | tf_op jit(solution)/shard_map/ppermute | solution.py:213
  66.3 21.8 %collective-permute-done.5.theirs_ref = bf16[2,2,256,128]{3,2,1,0:T(8,128)(2,1)S(1)} collective-permute-done((bf16[2,2,256,128]{3,2,1,0:T(8,128)(2,1)S(1)}, bf16[2,2,256,128]{3,2,1,0:T(8,128)(2,1)S(1)}, u32[]{:S(2)}, u32[]{:S(2)}) %collective-permute-start.5) | collective-permute-done | bytes 262176 | tf_op jit(solution)/shard_map/ppermute | solution.py:213
  88.1 0.4 trace.4.before_ref
  88.5 5.2 %collective-permute-done.4.theirs_ref = bf16[2,2,256,128]{3,2,1,0:T(8,128)(2,1)S(1)} collective-permute-done((bf16[2,2,256,128]{3,2,1,0:T(8,128)(2,1)S(1)}, bf16[2,2,256,128]{3,2,1,0:T(8,128)(2,1)S(1)}, u32[]{:S(2)}, u32[]{:S(2)}) %collective-permute-start.4) | collective-permute-done | bytes 262176 | tf_op jit(solution)/shard_map/ppermute | solution.py:213
  93.7 0.4 trace.5.before_ref
  94.1 5.2 %collective-permute-done.3.theirs_ref = bf16[2,2,256,128]{3,2,1,0:T(8,128)(2,1)S(1)} collective-permute-done((bf16[2,2,256,128]{3,2,1,0:T(8,128)(2,1)S(1)}, bf16[2,2,256,128]{3,2,1,0:T(8,128)(2,1)S(1)}, u32[]{:S(2)}, u32[]{:S(2)}) %collective-permute-start.3) | collective-permute-done | bytes 262176 | tf_op jit(solution)/shard_map/ppermute | solution.py:213
  99.3 0.4 trace.6.before_ref
  99.7 5.2 %collective-permute-done.2.theirs_ref = bf16[2,2,256,128]{3,2,1,0:T(8,128)(2,1)S(1)} collective-permute-done((bf16[2,2,256,128]{3,2,1,0:T(8,128)(2,1)S(1)}, bf16[2,2,256,128]{3,2,1,0:T(8,128)(2,1)S(1)}, u32[]{:S(2)}, u32[]{:S(2)}) %collective-permute-start.2) | collective-permute-done | bytes 262176 | tf_op jit(solution)/shard_map/ppermute | solution.py:213
  104.9 0.4 trace.7
  105.4 0.1 collective-permute-start.6
  105.4 0.6 collective-permute-start.7
  106.0 2.8 %collective-permute-done.6 = f32[1,2]{1,0:T(1,128)S(1)} collective-permute-done((f32[1,2]{1,0:T(1,128)S(1)}, f32[1,2]{1,0:T(1,128)S(1)}, u32[]{:S(2)}, u32[]{:S(2)}) %collective-permute-start.6) | collective-permute-done | bytes 40 | tf_op jit(solution)/shard_map/ppermute | solution.py:213
  108.7 1.6 %collective-permute-start.8 = (f32[1,2]{1,0:T(1,128)S(1)}, f32[1,2]{1,0:T(1,128)S(1)}, u32[]{:S(2)}, u32[]{:S(2)}) collective-permute-start(f32[1,2]{1,0:T(1,128)S(1)} %collective-permute-done.6), channel_id=1, source_target_pairs={{0,1},{1,0},{2,3},{3,2},{4,5},{5,4},{6,7},{7,6},{8,9},{9,8},{10,11... | collective-permute-start | bytes 32 | tf_op jit(solution)/shard_map/ppermute | solution.py:216
  110.4 0.0 collective-permute-done.7
  110.4 0.8 collective-permute-done.8
  111.2 0.5 add_add_fusion
  (4 shorter events, 0.0 us)
Async XLA Ops:
  0.0 42.6 %copy-start = (s32[16,24]{1,0:T(8,128)S(1)}, s32[16,24]{1,0:T(8,128)}, u32[]{:S(2)}) copy-start(s32[16,24]{1,0:T(8,128)} %param.9) | copy-start | bytes 4612
  4.2 7.7 %copy-start.2 = (s32[16]{0:T(128)S(1)}, s32[16]{0:T(128)}, u32[]{:S(2)}) copy-start(s32[16]{0:T(128)} %param.11) | copy-start | bytes 196
  4.2 48.1 %collective-permute-start.1 = (bf16[4,2,1024,128]{3,2,1,0:T(8,128)(2,1)}, bf16[4,2,1024,128]{3,2,1,0:T(8,128)(2,1)}, u32[]{:S(2)}, u32[]{:S(2)}) collective-permute-start(bf16[4,2,1024,128]{3,2,1,0:T(8,128)(2,1)} %sort.1.refs_2_), channel_id=1, source_target_pairs={{0,1},{1,0},{2,3},{3,2},{4,5},{5,4},{6,7},{7,6},{8,9},{9,8},{10,11... | collective-permute-start | bytes 6291464 | tf_op jit(solution)/shard_map/ppermute | solution.py:216
  7.3 30.1 %all-to-all-start.1 = ((bf16[8,8,2,2048]{3,2,1,0:T(2,128)(2,1)}), bf16[8,8,2,2048]{3,2,1,0:T(2,128)(2,1)S(1)}, u32[]{:S(2)}, u32[]{:S(2)}) async-start(bf16[8,8,2,2048]{3,2,1,0:T(2,128)(2,1)} %get-tuple-element.18), calls=%async_computation.1 | async-start | bytes 1048576 | tf_op jit(solution)/shard_map/all_to_all | solution.py:220
  11.9 25.5 %collective-permute-start = (bf16[8,8,2,2048]{3,2,1,0:T(2,128)(2,1)}, bf16[8,8,2,2048]{3,2,1,0:T(2,128)(2,1)}, u32[]{:S(2)}, u32[]{:S(2)}) collective-permute-start(bf16[8,8,2,2048]{3,2,1,0:T(2,128)(2,1)} %get-tuple-element.15), channel_id=1, source_target_pairs={{0,16},{1,17},{2,18},{3,19},{4,20},{5,21},{6,22},{7,23},{8,24},{9,... | collective-permute-start | bytes 1572872 | tf_op jit(solution)/shard_map/ppermute | solution.py:213
  37.4 12.7 %all-to-all-start = ((bf16[8,8,2,2048]{3,2,1,0:T(2,128)(2,1)}), bf16[8,8,2,2048]{3,2,1,0:T(2,128)(2,1)S(1)}, u32[]{:S(2)}, u32[]{:S(2)}) async-start(bf16[8,8,2,2048]{3,2,1,0:T(2,128)(2,1)} %collective-permute-done), calls=%async_computation | async-start | bytes 1048576 | tf_op jit(solution)/shard_map/all_to_all | solution.py:220
  43.9 8.4 %copy-start.1 = (bf16[4,2,1024,128]{3,2,1,0:T(8,128)(2,1)S(1)}, bf16[4,2,1024,128]{3,2,1,0:T(8,128)(2,1)}, u32[]{:S(2)}) copy-start(bf16[4,2,1024,128]{3,2,1,0:T(8,128)(2,1)} %sort.1.refs_2_) | copy-start | bytes 6291460
  56.6 31.5 %collective-permute-start.5 = (bf16[2,2,256,128]{3,2,1,0:T(8,128)(2,1)S(1)}, bf16[2,2,256,128]{3,2,1,0:T(8,128)(2,1)S(1)}, u32[]{:S(2)}, u32[]{:S(2)}) collective-permute-start(bf16[2,2,256,128]{3,2,1,0:T(8,128)(2,1)S(1)} %get-tuple-element.24), channel_id=1, source_target_pairs={{0,16},{1,17},{2,18},{3,19},{4,20},{5,21},{6,22},{7,23},{8,24},{9,... | collective-permute-start | bytes 786440 | tf_op jit(solution)/shard_map/ppermute | solution.py:213
  56.7 37.0 %collective-permute-start.4 = (bf16[2,2,256,128]{3,2,1,0:T(8,128)(2,1)S(1)}, bf16[2,2,256,128]{3,2,1,0:T(8,128)(2,1)S(1)}, u32[]{:S(2)}, u32[]{:S(2)}) collective-permute-start(bf16[2,2,256,128]{3,2,1,0:T(8,128)(2,1)S(1)} %get-tuple-element.22), channel_id=1, source_target_pairs={{0,17},{1,16},{2,19},{3,18},{4,21},{5,20},{6,23},{7,22},{8,25},{9,... | collective-permute-start | bytes 786440 | tf_op jit(solution)/shard_map/ppermute | solution.py:213
  59.7 39.6 %collective-permute-start.3 = (bf16[2,2,256,128]{3,2,1,0:T(8,128)(2,1)S(1)}, bf16[2,2,256,128]{3,2,1,0:T(8,128)(2,1)S(1)}, u32[]{:S(2)}, u32[]{:S(2)}) collective-permute-start(bf16[2,2,256,128]{3,2,1,0:T(8,128)(2,1)S(1)} %get-tuple-element.20), channel_id=1, source_target_pairs={{0,16},{1,17},{2,18},{3,19},{4,20},{5,21},{6,22},{7,23},{8,24},{9,... | collective-permute-start | bytes 786440 | tf_op jit(solution)/shard_map/ppermute | solution.py:213
  64.0 40.9 %collective-permute-start.2 = (bf16[2,2,256,128]{3,2,1,0:T(8,128)(2,1)S(1)}, bf16[2,2,256,128]{3,2,1,0:T(8,128)(2,1)S(1)}, u32[]{:S(2)}, u32[]{:S(2)}) collective-permute-start(bf16[2,2,256,128]{3,2,1,0:T(8,128)(2,1)S(1)} %get-tuple-element.17), channel_id=1, source_target_pairs={{0,16},{1,17},{2,18},{3,19},{4,20},{5,21},{6,22},{7,23},{8,24},{9,... | collective-permute-start | bytes 786440 | tf_op jit(solution)/shard_map/ppermute | solution.py:213
  105.4 3.4 %collective-permute-start.6 = (f32[1,2]{1,0:T(1,128)S(1)}, f32[1,2]{1,0:T(1,128)S(1)}, u32[]{:S(2)}, u32[]{:S(2)}) collective-permute-start(f32[1,2]{1,0:T(1,128)S(1)} %trace.7), channel_id=1, source_target_pairs={{0,16},{1,17},{2,18},{3,19},{4,20},{5,21},{6,22},{7,23},{8,24},{9,... | collective-permute-start | bytes 32 | tf_op jit(solution)/shard_map/ppermute | solution.py:213
  105.4 4.9 %collective-permute-start.7 = (f32[1,2]{1,0:T(1,128)S(1)}, f32[1,2]{1,0:T(1,128)S(1)}, u32[]{:S(2)}, u32[]{:S(2)}) collective-permute-start(f32[1,2]{1,0:T(1,128)S(1)} %trace.7), channel_id=1, source_target_pairs={{0,1},{1,0},{2,3},{3,2},{4,5},{5,4},{6,7},{7,6},{8,9},{9,8},{10,11... | collective-permute-start | bytes 32 | tf_op jit(solution)/shard_map/ppermute | solution.py:216
  108.7 2.5 %collective-permute-start.8 = (f32[1,2]{1,0:T(1,128)S(1)}, f32[1,2]{1,0:T(1,128)S(1)}, u32[]{:S(2)}, u32[]{:S(2)}) collective-permute-start(f32[1,2]{1,0:T(1,128)S(1)} %collective-permute-done.6), channel_id=1, source_target_pairs={{0,1},{1,0},{2,3},{3,2},{4,5},{5,4},{6,7},{7,6},{8,9},{9,8},{10,11... | collective-permute-start | bytes 32 | tf_op jit(solution)/shard_map/ppermute | solution.py:216

commit v2 on v1

--- a/solution.py
+++ b/solution.py
@@ -121,18 +121,23 @@
     combine(ns, weight_ref, elem_ref, phi)
     width = held.shape[-1]
     dot = functools.partial(jnp.dot, preferred_element_type=F32)
-    for n, out in enumerate(outs):
-        for load in loads[n]:
+    for n in range(0, len(outs), 2):
+        for load in (*loads[n], *loads[n + 1]):
             load.wait()
         prop_real, prop_imag = (
-            jnp.concatenate([held[n, 0, c], held[n, 1, c]], axis=1) for c in range(2)
+            jnp.concatenate([held[m, place, c] for m in (n, n + 1) for place in range(2)], axis=1)
+            for c in range(2)
         )
-        real = dot(phi[0], prop_real) - dot(phi[1], prop_imag)
-        imag = dot(phi[0], prop_imag) + dot(phi[1], prop_real)
-        for place in range(2):
-            part = slice(place * width, (place + 1) * width)
-            out[place, 0] = real[:, part].astype(BF16)
-            out[place, 1] = imag[:, part].astype(BF16)
+        step = outs[n].shape[2] // 2
+        for first in range(0, outs[n].shape[2], step):
+            span = slice(first, first + step)
+            real = dot(phi[0, span], prop_real) - dot(phi[1, span], prop_imag)
+            imag = dot(phi[0, span], prop_imag) + dot(phi[1, span], prop_real)
+            for m in range(4):
+                part = slice(m * width, (m + 1) * width)
+                out = outs[n + m // 2]
+                out[m % 2, 0, span] = real[:, part].astype(BF16)
+                out[m % 2, 1, span] = imag[:, part].astype(BF16)
 
 
 def dress(stage, weight, elem, own, other, ns):
@@ -160,19 +165,18 @@
 
 def trace_kernel(mine_ref, theirs_ref, before_ref, out_ref):
     width = mine_ref.shape[-1]
-    real = imag = None
+    left, right = ([], []), []
     for block in range(2):
         span = slice(block * width, (block + 1) * width)
-        left = [
-            jnp.concatenate([mine_ref[0, c, span, :], mine_ref[1, c, span, :]], axis=1)
-            for c in range(2)
-        ]
-        right = [theirs_ref[block, c] for c in range(2)]
-        dot = functools.partial(jnp.dot, preferred_element_type=F32)
-        re = dot(left[0], right[0]) - dot(left[1], right[1])
-        im = dot(left[0], right[1]) + dot(left[1], right[0])
-        real = re if real is None else real + re
-        imag = im if imag is None else imag + im
+        for c in range(2):
+            left[c].extend(mine_ref[place, c, span, :] for place in range(2))
+        right.append(jnp.concatenate([theirs_ref[block, c] for c in range(2)], axis=1))
+    right = jnp.concatenate(right, axis=0)
+    by_real, by_imag = (
+        jnp.dot(jnp.concatenate(part, axis=1), right, preferred_element_type=F32) for part in left
+    )
+    real = by_real[:, :width] - by_imag[:, width:]
+    imag = by_real[:, width:] + by_imag[:, :width]
     shape = real.shape
     diagonal = lax.broadcasted_iota(jnp.int32, shape, 0) == lax.broadcasted_iota(jnp.int32, shape, 1)
     real = jnp.sum(jnp.where(diagonal, real, 0.0))
@@ -190,7 +194,7 @@
         cost_estimate=pl.CostEstimate(
             flops=8 * mine.shape[2] ** 3, bytes_accessed=4 * mine.size, transcendentals=0
         ),
-        compiler_params=pltpu.CompilerParams(vmem_limit_bytes=4 * MIB),
+        compiler_params=pltpu.CompilerParams(vmem_limit_bytes=2 * MIB),
         name="trace",
     )(mine, theirs, before)
 

time: 112 us -> 112 us (level)
  no operation moved by 1% of the time
where the time goes in v2:
time: 112 us; the launch traced here: 111 us
  waiting for transfers between devices  70.3 us (63%)
  starting transfers between devices  17.5 us (16%)
  Pallas kernels  15.8 us (14%)
  local copies, waits for them, and re-layouts  5.22 us (5%)
  other arithmetic  2.24 us (2%)
    ppermute x6, waiting for transfers between devices, across(): return lax.ppermute(value, ('pair', 'blk'), moves)  65.5 us
    all_to_all x2, starting transfers between devices, within(): lax.all_to_all(value, 'pair', 0, 0, axis_index_groups=groups, tiled=True)  9.15 us
    pallas_call x2, Pallas kernels, dress(): pl.pallas_call(functools.partial(dress_kernel, ns, stage), out_shape=[blo...  7.71 us
    ppermute x6, starting transfers between devices, across(): return lax.ppermute(value, ('pair', 'blk'), moves)  5.53 us
    reshape x4, local copies, waits for them, and re-layouts, rows_of(): shaped = received.reshape(half, nop, 2, rows, nv)  4.44 us
    pallas_call x1, Pallas kernels, sort(): pl.pallas_call(functools.partial(sort_kernel, half, rows, nv), out_shape=...  4.23 us
    all_to_all x2, waiting for transfers between devices, within(): lax.all_to_all(value, 'pair', 0, 0, axis_index_groups=groups, tiled=True)  3.96 us
    ppermute x3, starting transfers between devices, beside(): return lax.ppermute(value, 'blk', [(0, 1), (1, 0)])  2.87 us
  transfers between devices with their start and end apart: 11, of which 8 were waited for; matrix products, arithmetic and copies ran while one was open for 6% of the time, Pallas kernels for 7%

profile of v2, /device:TPU:27, one launch (start us, length us, event | category | flops | bytes accessed | tf_op | source)
XLA Modules:
  0.0 111.2 jit_solution(5583405635616040858)
XLA Ops:
  0.0 0.0 copy-start
  0.0 4.2 %sort.1.refs_2_ = bf16[4,2,1024,128]{3,2,1,0:T(8,128)(2,1)} custom-call(bf16[2,1024,512]{2,1,0:T(8,128)(2,1)} %bitcast.22), custom_call_target="tpu_custom_call" | custom-call | flops 1073741824 | bytes 4194304 | tf_op jit(solution)/shard_map/sort/pallas_call | solution.py:70
  4.2 0.0 copy-start.2
  4.2 0.7 collective-permute-start.1
  4.9 2.4 %pick.1 = (bf16[8,8,2,2048]{3,2,1,0:T(2,128)(2,1)}, bf16[8,8,2,2048]{3,2,1,0:T(2,128)(2,1)}) custom-call(s32[2,16]{1,0:T(2,128)} %bitcast.24, bf16[16,8,2,2048]{3,2,1,0:T(2,128)(2,1)} %table_ref.1), custom_call_target="tpu_custom_call" | custom-call | bytes 2097152 | tf_op jit(solution)/shard_map/pick/pallas_call | solution.py:35
  7.3 4.6 %all-to-all-start.1 = ((bf16[8,8,2,2048]{3,2,1,0:T(2,128)(2,1)}), bf16[8,8,2,2048]{3,2,1,0:T(2,128)(2,1)S(1)}, u32[]{:S(2)}, u32[]{:S(2)}) async-start(bf16[8,8,2,2048]{3,2,1,0:T(2,128)(2,1)} %get-tuple-element.18), calls=%async_computation.1 | async-start | bytes 1048576 | tf_op jit(solution)/shard_map/all_to_all | solution.py:224
  11.9 0.1 collective-permute-start
  12.0 0.0 copy-done.2
  12.0 0.6 dynamic_slice.10
  12.6 24.8 %collective-permute-done = bf16[8,8,2,2048]{3,2,1,0:T(2,128)(2,1)} collective-permute-done((bf16[8,8,2,2048]{3,2,1,0:T(2,128)(2,1)}, bf16[8,8,2,2048]{3,2,1,0:T(2,128)(2,1)}, u32[]{:S(2)}, u32[]{:S(2)}) %collective-permute-start) | collective-permute-done | bytes 524320 | tf_op jit(solution)/shard_map/ppermute | solution.py:217
  37.4 0.0 all-to-all-done.1
  37.4 4.5 %all-to-all-start = ((bf16[8,8,2,2048]{3,2,1,0:T(2,128)(2,1)}), bf16[8,8,2,2048]{3,2,1,0:T(2,128)(2,1)S(1)}, u32[]{:S(2)}, u32[]{:S(2)}) async-start(bf16[8,8,2,2048]{3,2,1,0:T(2,128)(2,1)} %collective-permute-done), calls=%async_computation | async-start | bytes 1048576 | tf_op jit(solution)/shard_map/all_to_all | solution.py:224
  41.9 0.6 iota_compare_fusion.1
  42.6 0.0 copy-done
  42.6 0.7 select_bitcast_fusion
  43.3 0.4 select_reduce_fusion
  43.7 0.1 broadcast_in_dim.47
  43.8 0.1 reshape.44.refs_0_
  43.9 0.0 copy-start.1
  43.9 1.1 %reshape.47 = bf16[8,8,2,8,256]{4,3,2,1,0:T(8,128)(2,1)} reshape(bf16[8,8,2,2048]{3,2,1,0:T(2,128)(2,1)S(1)} %all-to-all-done.1) | data formatting | bytes 1048576 | tf_op jit(solution)/shard_map/reshape | solution.py:227
  45.0 1.1 copy.14
  46.1 4.0 %all-to-all-done = bf16[8,8,2,2048]{3,2,1,0:T(2,128)(2,1)S(1)} async-done(((bf16[8,8,2,2048]{3,2,1,0:T(2,128)(2,1)}), bf16[8,8,2,2048]{3,2,1,0:T(2,128)(2,1)S(1)}, u32[]{:S(2)}, u32[]{:S(2)}) %all-to-all-start) | async-done | bytes 524320 | tf_op jit(solution)/shard_map/all_to_all | solution.py:224
  50.1 1.1 %reshape.45 = bf16[8,8,2,8,256]{4,3,2,1,0:T(8,128)(2,1)} reshape(bf16[8,8,2,2048]{3,2,1,0:T(2,128)(2,1)S(1)} %all-to-all-done) | data formatting | bytes 1048576 | tf_op jit(solution)/shard_map/reshape | solution.py:227
  51.2 1.1 copy.15
  52.3 0.0 collective-permute-done.1.refs_3_
  52.3 0.0 copy-done.1
  52.3 3.9 %shard_map.65 = (bf16[2,2,256,128]{3,2,1,0:T(8,128)(2,1)S(1)}, bf16[2,2,256,128]{3,2,1,0:T(8,128)(2,1)S(1)}, bf16[2,2,256,128]{3,2,1,0:T(8,128)(2,1)S(1)}, bf16[2,2,256,128]{3,2,1,0:T(8,128)(2,1)S(1)}) custom-call(f32[16,256]{1,0:T(8,128)S(1)} %reshape.44.refs_0_, bf16[8,2,64,256]{3,2,1,0:T(8,128)(2,1)S(1)} %bitcast.21, ...), custom_call_target="tpu_custom_call" | custom-call | flops 2147483648 | bytes 4194304 | tf_op jit(solution)/shard_map/pallas_call | solution.py:147
  56.2 0.1 collective-permute-start.5
  56.3 3.0 %collective-permute-start.4 = (bf16[2,2,256,128]{3,2,1,0:T(8,128)(2,1)S(1)}, bf16[2,2,256,128]{3,2,1,0:T(8,128)(2,1)S(1)}, u32[]{:S(2)}, u32[]{:S(2)}) collective-permute-start(bf16[2,2,256,128]{3,2,1,0:T(8,128)(2,1)S(1)} %get-tuple-element.22), channel_id=1, source_target_pairs={{0,17},{1,16},{2,19},{3,18},{4,21},{5,20},{6,23},{7,22},{8,25},{9,... | collective-permute-start | bytes 786440 | tf_op jit(solution)/shard_map/ppermute | solution.py:217
  59.3 0.0 collective-permute-start.3
  59.3 3.8 %shard_map.64 = (bf16[2,2,256,128]{3,2,1,0:T(8,128)(2,1)S(1)}, bf16[2,2,256,128]{3,2,1,0:T(8,128)(2,1)S(1)}, bf16[2,2,256,128]{3,2,1,0:T(8,128)(2,1)S(1)}, bf16[2,2,256,128]{3,2,1,0:T(8,128)(2,1)S(1)}) custom-call(f32[16,256]{1,0:T(8,128)S(1)} %reshape.44.refs_0_, bf16[8,2,64,256]{3,2,1,0:T(8,128)(2,1)S(1)} %bitcast.20, ...), custom_call_target="tpu_custom_call" | custom-call | flops 2147483648 | bytes 4194304 | tf_op jit(solution)/shard_map/pallas_call | solution.py:147
  63.1 2.3 %collective-permute-start.2 = (bf16[2,2,256,128]{3,2,1,0:T(8,128)(2,1)S(1)}, bf16[2,2,256,128]{3,2,1,0:T(8,128)(2,1)S(1)}, u32[]{:S(2)}, u32[]{:S(2)}) collective-permute-start(bf16[2,2,256,128]{3,2,1,0:T(8,128)(2,1)S(1)} %get-tuple-element.17), channel_id=1, source_target_pairs={{0,16},{1,17},{2,18},{3,19},{4,20},{5,21},{6,22},{7,23},{8,24},{9,... | collective-permute-start | bytes 786440 | tf_op jit(solution)/shard_map/ppermute | solution.py:217
  65.4 22.2 %collective-permute-done.5.theirs_ref = bf16[2,2,256,128]{3,2,1,0:T(8,128)(2,1)S(1)} collective-permute-done((bf16[2,2,256,128]{3,2,1,0:T(8,128)(2,1)S(1)}, bf16[2,2,256,128]{3,2,1,0:T(8,128)(2,1)S(1)}, u32[]{:S(2)}, u32[]{:S(2)}) %collective-permute-start.5) | collective-permute-done | bytes 262176 | tf_op jit(solution)/shard_map/ppermute | solution.py:217
  87.7 0.4 trace.4.before_ref
  88.0 5.3 %collective-permute-done.4.theirs_ref = bf16[2,2,256,128]{3,2,1,0:T(8,128)(2,1)S(1)} collective-permute-done((bf16[2,2,256,128]{3,2,1,0:T(8,128)(2,1)S(1)}, bf16[2,2,256,128]{3,2,1,0:T(8,128)(2,1)S(1)}, u32[]{:S(2)}, u32[]{:S(2)}) %collective-permute-start.4) | collective-permute-done | bytes 262176 | tf_op jit(solution)/shard_map/ppermute | solution.py:217
  93.3 0.4 trace.5.before_ref
  93.6 5.3 %collective-permute-done.3.theirs_ref = bf16[2,2,256,128]{3,2,1,0:T(8,128)(2,1)S(1)} collective-permute-done((bf16[2,2,256,128]{3,2,1,0:T(8,128)(2,1)S(1)}, bf16[2,2,256,128]{3,2,1,0:T(8,128)(2,1)S(1)}, u32[]{:S(2)}, u32[]{:S(2)}) %collective-permute-start.3) | collective-permute-done | bytes 262176 | tf_op jit(solution)/shard_map/ppermute | solution.py:217
  98.9 0.4 trace.6.before_ref
  99.3 5.3 %collective-permute-done.2.theirs_ref = bf16[2,2,256,128]{3,2,1,0:T(8,128)(2,1)S(1)} collective-permute-done((bf16[2,2,256,128]{3,2,1,0:T(8,128)(2,1)S(1)}, bf16[2,2,256,128]{3,2,1,0:T(8,128)(2,1)S(1)}, u32[]{:S(2)}, u32[]{:S(2)}) %collective-permute-start.2) | collective-permute-done | bytes 262176 | tf_op jit(solution)/shard_map/ppermute | solution.py:217
  104.5 0.4 trace.7
  104.9 0.1 collective-permute-start.6
  105.0 0.6 collective-permute-start.7
  105.5 2.8 %collective-permute-done.6 = f32[1,2]{1,0:T(1,128)S(1)} collective-permute-done((f32[1,2]{1,0:T(1,128)S(1)}, f32[1,2]{1,0:T(1,128)S(1)}, u32[]{:S(2)}, u32[]{:S(2)}) %collective-permute-start.6) | collective-permute-done | bytes 40 | tf_op jit(solution)/shard_map/ppermute | solution.py:217
  108.3 1.6 %collective-permute-start.8 = (f32[1,2]{1,0:T(1,128)S(1)}, f32[1,2]{1,0:T(1,128)S(1)}, u32[]{:S(2)}, u32[]{:S(2)}) collective-permute-start(f32[1,2]{1,0:T(1,128)S(1)} %collective-permute-done.6), channel_id=1, source_target_pairs={{0,1},{1,0},{2,3},{3,2},{4,5},{5,4},{6,7},{7,6},{8,9},{9,8},{10,11... | collective-permute-start | bytes 32 | tf_op jit(solution)/shard_map/ppermute | solution.py:220
  109.9 0.0 collective-permute-done.7
  109.9 0.8 collective-permute-done.8
  110.7 0.5 add_add_fusion
  (4 shorter events, 0.0 us)
Async XLA Ops:
  0.0 42.6 %copy-start = (s32[16,24]{1,0:T(8,128)S(1)}, s32[16,24]{1,0:T(8,128)}, u32[]{:S(2)}) copy-start(s32[16,24]{1,0:T(8,128)} %param.9) | copy-start | bytes 4612
  4.2 7.7 %copy-start.2 = (s32[16]{0:T(128)S(1)}, s32[16]{0:T(128)}, u32[]{:S(2)}) copy-start(s32[16]{0:T(128)} %param.11) | copy-start | bytes 196
  4.2 48.1 %collective-permute-start.1 = (bf16[4,2,1024,128]{3,2,1,0:T(8,128)(2,1)}, bf16[4,2,1024,128]{3,2,1,0:T(8,128)(2,1)}, u32[]{:S(2)}, u32[]{:S(2)}) collective-permute-start(bf16[4,2,1024,128]{3,2,1,0:T(8,128)(2,1)} %sort.1.refs_2_), channel_id=1, source_target_pairs={{0,1},{1,0},{2,3},{3,2},{4,5},{5,4},{6,7},{7,6},{8,9},{9,8},{10,11... | collective-permute-start | bytes 6291464 | tf_op jit(solution)/shard_map/ppermute | solution.py:220
  7.3 30.1 %all-to-all-start.1 = ((bf16[8,8,2,2048]{3,2,1,0:T(2,128)(2,1)}), bf16[8,8,2,2048]{3,2,1,0:T(2,128)(2,1)S(1)}, u32[]{:S(2)}, u32[]{:S(2)}) async-start(bf16[8,8,2,2048]{3,2,1,0:T(2,128)(2,1)} %get-tuple-element.18), calls=%async_computation.1 | async-start | bytes 1048576 | tf_op jit(solution)/shard_map/all_to_all | solution.py:224
  11.9 25.5 %collective-permute-start = (bf16[8,8,2,2048]{3,2,1,0:T(2,128)(2,1)}, bf16[8,8,2,2048]{3,2,1,0:T(2,128)(2,1)}, u32[]{:S(2)}, u32[]{:S(2)}) collective-permute-start(bf16[8,8,2,2048]{3,2,1,0:T(2,128)(2,1)} %get-tuple-element.15), channel_id=1, source_target_pairs={{0,16},{1,17},{2,18},{3,19},{4,20},{5,21},{6,22},{7,23},{8,24},{9,... | collective-permute-start | bytes 1572872 | tf_op jit(solution)/shard_map/ppermute | solution.py:217
  37.4 12.7 %all-to-all-start = ((bf16[8,8,2,2048]{3,2,1,0:T(2,128)(2,1)}), bf16[8,8,2,2048]{3,2,1,0:T(2,128)(2,1)S(1)}, u32[]{:S(2)}, u32[]{:S(2)}) async-start(bf16[8,8,2,2048]{3,2,1,0:T(2,128)(2,1)} %collective-permute-done), calls=%async_computation | async-start | bytes 1048576 | tf_op jit(solution)/shard_map/all_to_all | solution.py:224
  43.9 8.4 %copy-start.1 = (bf16[4,2,1024,128]{3,2,1,0:T(8,128)(2,1)S(1)}, bf16[4,2,1024,128]{3,2,1,0:T(8,128)(2,1)}, u32[]{:S(2)}) copy-start(bf16[4,2,1024,128]{3,2,1,0:T(8,128)(2,1)} %sort.1.refs_2_) | copy-start | bytes 6291460
  56.2 31.5 %collective-permute-start.5 = (bf16[2,2,256,128]{3,2,1,0:T(8,128)(2,1)S(1)}, bf16[2,2,256,128]{3,2,1,0:T(8,128)(2,1)S(1)}, u32[]{:S(2)}, u32[]{:S(2)}) collective-permute-start(bf16[2,2,256,128]{3,2,1,0:T(8,128)(2,1)S(1)} %get-tuple-element.24), channel_id=1, source_target_pairs={{0,16},{1,17},{2,18},{3,19},{4,20},{5,21},{6,22},{7,23},{8,24},{9,... | collective-permute-start | bytes 786440 | tf_op jit(solution)/shard_map/ppermute | solution.py:217
  56.3 37.0 %collective-permute-start.4 = (bf16[2,2,256,128]{3,2,1,0:T(8,128)(2,1)S(1)}, bf16[2,2,256,128]{3,2,1,0:T(8,128)(2,1)S(1)}, u32[]{:S(2)}, u32[]{:S(2)}) collective-permute-start(bf16[2,2,256,128]{3,2,1,0:T(8,128)(2,1)S(1)} %get-tuple-element.22), channel_id=1, source_target_pairs={{0,17},{1,16},{2,19},{3,18},{4,21},{5,20},{6,23},{7,22},{8,25},{9,... | collective-permute-start | bytes 786440 | tf_op jit(solution)/shard_map/ppermute | solution.py:217
  59.3 39.6 %collective-permute-start.3 = (bf16[2,2,256,128]{3,2,1,0:T(8,128)(2,1)S(1)}, bf16[2,2,256,128]{3,2,1,0:T(8,128)(2,1)S(1)}, u32[]{:S(2)}, u32[]{:S(2)}) collective-permute-start(bf16[2,2,256,128]{3,2,1,0:T(8,128)(2,1)S(1)} %get-tuple-element.20), channel_id=1, source_target_pairs={{0,16},{1,17},{2,18},{3,19},{4,20},{5,21},{6,22},{7,23},{8,24},{9,... | collective-permute-start | bytes 786440 | tf_op jit(solution)/shard_map/ppermute | solution.py:217
  63.1 41.4 %collective-permute-start.2 = (bf16[2,2,256,128]{3,2,1,0:T(8,128)(2,1)S(1)}, bf16[2,2,256,128]{3,2,1,0:T(8,128)(2,1)S(1)}, u32[]{:S(2)}, u32[]{:S(2)}) collective-permute-start(bf16[2,2,256,128]{3,2,1,0:T(8,128)(2,1)S(1)} %get-tuple-element.17), channel_id=1, source_target_pairs={{0,16},{1,17},{2,18},{3,19},{4,20},{5,21},{6,22},{7,23},{8,24},{9,... | collective-permute-start | bytes 786440 | tf_op jit(solution)/shard_map/ppermute | solution.py:217
  104.9 3.4 %collective-permute-start.6 = (f32[1,2]{1,0:T(1,128)S(1)}, f32[1,2]{1,0:T(1,128)S(1)}, u32[]{:S(2)}, u32[]{:S(2)}) collective-permute-start(f32[1,2]{1,0:T(1,128)S(1)} %trace.7), channel_id=1, source_target_pairs={{0,16},{1,17},{2,18},{3,19},{4,20},{5,21},{6,22},{7,23},{8,24},{9,... | collective-permute-start | bytes 32 | tf_op jit(solution)/shard_map/ppermute | solution.py:217
  105.0 4.9 %collective-permute-start.7 = (f32[1,2]{1,0:T(1,128)S(1)}, f32[1,2]{1,0:T(1,128)S(1)}, u32[]{:S(2)}, u32[]{:S(2)}) collective-permute-start(f32[1,2]{1,0:T(1,128)S(1)} %trace.7), channel_id=1, source_target_pairs={{0,1},{1,0},{2,3},{3,2},{4,5},{5,4},{6,7},{7,6},{8,9},{9,8},{10,11... | collective-permute-start | bytes 32 | tf_op jit(solution)/shard_map/ppermute | solution.py:220
  108.3 2.5 %collective-permute-start.8 = (f32[1,2]{1,0:T(1,128)S(1)}, f32[1,2]{1,0:T(1,128)S(1)}, u32[]{:S(2)}, u32[]{:S(2)}) collective-permute-start(f32[1,2]{1,0:T(1,128)S(1)} %collective-permute-done.6), channel_id=1, source_target_pairs={{0,1},{1,0},{2,3},{3,2},{4,5},{5,4},{6,7},{7,6},{8,9},{9,8},{10,11... | collective-permute-start | bytes 32 | tf_op jit(solution)/shard_map/ppermute | solution.py:220

commit v3 on v2

--- a/solution.py
+++ b/solution.py
@@ -165,18 +165,19 @@
 
 def trace_kernel(mine_ref, theirs_ref, before_ref, out_ref):
     width = mine_ref.shape[-1]
-    left, right = ([], []), []
+    real = imag = None
     for block in range(2):
         span = slice(block * width, (block + 1) * width)
-        for c in range(2):
-            left[c].extend(mine_ref[place, c, span, :] for place in range(2))
-        right.append(jnp.concatenate([theirs_ref[block, c] for c in range(2)], axis=1))
-    right = jnp.concatenate(right, axis=0)
-    by_real, by_imag = (
-        jnp.dot(jnp.concatenate(part, axis=1), right, preferred_element_type=F32) for part in left
-    )
-    real = by_real[:, :width] - by_imag[:, width:]
-    imag = by_real[:, width:] + by_imag[:, :width]
+        left = [
+            jnp.concatenate([mine_ref[0, c, span, :], mine_ref[1, c, span, :]], axis=1)
+            for c in range(2)
+        ]
+        right = [theirs_ref[block, c] for c in range(2)]
+        dot = functools.partial(jnp.dot, preferred_element_type=F32)
+        re = dot(left[0], right[0]) - dot(left[1], right[1])
+        im = dot(left[0], right[1]) + dot(left[1], right[0])
+        real = re if real is None else real + re
+        imag = im if imag is None else imag + im
     shape = real.shape
     diagonal = lax.broadcasted_iota(jnp.int32, shape, 0) == lax.broadcasted_iota(jnp.int32, shape, 1)
     real = jnp.sum(jnp.where(diagonal, real, 0.0))

time: 112 us -> 112 us (level)
  no operation moved by 1% of the time
where the time goes in v3:
time: 112 us; the launch traced here: 111 us
  waiting for transfers between devices  70.1 us (63%)
  starting transfers between devices  17.5 us (16%)
  Pallas kernels  16 us (14%)
  local copies, waits for them, and re-layouts  5.22 us (5%)
  other arithmetic  2.24 us (2%)
    ppermute x6, waiting for transfers between devices, across(): return lax.ppermute(value, ('pair', 'blk'), moves)  65.4 us
    all_to_all x2, starting transfers between devices, within(): lax.all_to_all(value, 'pair', 0, 0, axis_index_groups=groups, tiled=True)  9.15 us
    pallas_call x2, Pallas kernels, dress(): pl.pallas_call(functools.partial(dress_kernel, ns, stage), out_shape=[blo...  7.71 us
    ppermute x6, starting transfers between devices, across(): return lax.ppermute(value, ('pair', 'blk'), moves)  5.53 us
    reshape x4, local copies, waits for them, and re-layouts, rows_of(): shaped = received.reshape(half, nop, 2, rows, nv)  4.44 us
    pallas_call x1, Pallas kernels, sort(): pl.pallas_call(functools.partial(sort_kernel, half, rows, nv), out_shape=...  4.23 us
    all_to_all x2, waiting for transfers between devices, within(): lax.all_to_all(value, 'pair', 0, 0, axis_index_groups=groups, tiled=True)  3.96 us
    ppermute x3, starting transfers between devices, beside(): return lax.ppermute(value, 'blk', [(0, 1), (1, 0)])  2.87 us
  transfers between devices with their start and end apart: 11, of which 8 were waited for; matrix products, arithmetic and copies ran while one was open for 6% of the time, Pallas kernels for 7%

profile of v3, /device:TPU:27, one launch (start us, length us, event | category | flops | bytes accessed | tf_op | source)
XLA Modules:
  0.0 111.3 jit_solution(11559469587350053666)
XLA Ops:
  0.0 0.0 copy-start
  0.0 4.2 %sort.1.refs_2_ = bf16[4,2,1024,128]{3,2,1,0:T(8,128)(2,1)} custom-call(bf16[2,1024,512]{2,1,0:T(8,128)(2,1)} %bitcast.22), custom_call_target="tpu_custom_call" | custom-call | flops 1073741824 | bytes 4194304 | tf_op jit(solution)/shard_map/sort/pallas_call | solution.py:70
  4.2 0.0 copy-start.2
  4.2 0.7 collective-permute-start.1
  4.9 2.4 %pick.1 = (bf16[8,8,2,2048]{3,2,1,0:T(2,128)(2,1)}, bf16[8,8,2,2048]{3,2,1,0:T(2,128)(2,1)}) custom-call(s32[2,16]{1,0:T(2,128)} %bitcast.24, bf16[16,8,2,2048]{3,2,1,0:T(2,128)(2,1)} %table_ref.1), custom_call_target="tpu_custom_call" | custom-call | bytes 2097152 | tf_op jit(solution)/shard_map/pick/pallas_call | solution.py:35
  7.3 4.6 %all-to-all-start.1 = ((bf16[8,8,2,2048]{3,2,1,0:T(2,128)(2,1)}), bf16[8,8,2,2048]{3,2,1,0:T(2,128)(2,1)S(1)}, u32[]{:S(2)}, u32[]{:S(2)}) async-start(bf16[8,8,2,2048]{3,2,1,0:T(2,128)(2,1)} %get-tuple-element.18), calls=%async_computation.1 | async-start | bytes 1048576 | tf_op jit(solution)/shard_map/all_to_all | solution.py:225
  11.9 0.1 collective-permute-start
  12.0 0.0 copy-done.2
  12.0 0.6 dynamic_slice.10
  12.6 24.8 %collective-permute-done = bf16[8,8,2,2048]{3,2,1,0:T(2,128)(2,1)} collective-permute-done((bf16[8,8,2,2048]{3,2,1,0:T(2,128)(2,1)}, bf16[8,8,2,2048]{3,2,1,0:T(2,128)(2,1)}, u32[]{:S(2)}, u32[]{:S(2)}) %collective-permute-start) | collective-permute-done | bytes 524320 | tf_op jit(solution)/shard_map/ppermute | solution.py:218
  37.4 0.0 all-to-all-done.1
  37.4 4.5 %all-to-all-start = ((bf16[8,8,2,2048]{3,2,1,0:T(2,128)(2,1)}), bf16[8,8,2,2048]{3,2,1,0:T(2,128)(2,1)S(1)}, u32[]{:S(2)}, u32[]{:S(2)}) async-start(bf16[8,8,2,2048]{3,2,1,0:T(2,128)(2,1)} %collective-permute-done), calls=%async_computation | async-start | bytes 1048576 | tf_op jit(solution)/shard_map/all_to_all | solution.py:225
  41.9 0.6 iota_compare_fusion.1
  42.6 0.0 copy-done
  42.6 0.7 select_bitcast_fusion
  43.3 0.4 select_reduce_fusion
  43.7 0.1 broadcast_in_dim.47
  43.8 0.1 reshape.44.refs_0_
  43.9 0.0 copy-start.1
  43.9 1.1 %reshape.47 = bf16[8,8,2,8,256]{4,3,2,1,0:T(8,128)(2,1)} reshape(bf16[8,8,2,2048]{3,2,1,0:T(2,128)(2,1)S(1)} %all-to-all-done.1) | data formatting | bytes 1048576 | tf_op jit(solution)/shard_map/reshape | solution.py:228
  45.0 1.1 copy.14
  46.1 4.0 %all-to-all-done = bf16[8,8,2,2048]{3,2,1,0:T(2,128)(2,1)S(1)} async-done(((bf16[8,8,2,2048]{3,2,1,0:T(2,128)(2,1)}), bf16[8,8,2,2048]{3,2,1,0:T(2,128)(2,1)S(1)}, u32[]{:S(2)}, u32[]{:S(2)}) %all-to-all-start) | async-done | bytes 524320 | tf_op jit(solution)/shard_map/all_to_all | solution.py:225
  50.1 1.1 %reshape.45 = bf16[8,8,2,8,256]{4,3,2,1,0:T(8,128)(2,1)} reshape(bf16[8,8,2,2048]{3,2,1,0:T(2,128)(2,1)S(1)} %all-to-all-done) | data formatting | bytes 1048576 | tf_op jit(solution)/shard_map/reshape | solution.py:228
  51.2 1.1 copy.15
  52.3 0.0 collective-permute-done.1.refs_3_
  52.3 0.0 copy-done.1
  52.3 3.9 %shard_map.65 = (bf16[2,2,256,128]{3,2,1,0:T(8,128)(2,1)S(1)}, bf16[2,2,256,128]{3,2,1,0:T(8,128)(2,1)S(1)}, bf16[2,2,256,128]{3,2,1,0:T(8,128)(2,1)S(1)}, bf16[2,2,256,128]{3,2,1,0:T(8,128)(2,1)S(1)}) custom-call(f32[16,256]{1,0:T(8,128)S(1)} %reshape.44.refs_0_, bf16[8,2,64,256]{3,2,1,0:T(8,128)(2,1)S(1)} %bitcast.21, ...), custom_call_target="tpu_custom_call" | custom-call | flops 2147483648 | bytes 4194304 | tf_op jit(solution)/shard_map/pallas_call | solution.py:147
  56.2 0.1 collective-permute-start.5
  56.3 3.0 %collective-permute-start.4 = (bf16[2,2,256,128]{3,2,1,0:T(8,128)(2,1)S(1)}, bf16[2,2,256,128]{3,2,1,0:T(8,128)(2,1)S(1)}, u32[]{:S(2)}, u32[]{:S(2)}) collective-permute-start(bf16[2,2,256,128]{3,2,1,0:T(8,128)(2,1)S(1)} %get-tuple-element.22), channel_id=1, source_target_pairs={{0,17},{1,16},{2,19},{3,18},{4,21},{5,20},{6,23},{7,22},{8,25},{9,... | collective-permute-start | bytes 786440 | tf_op jit(solution)/shard_map/ppermute | solution.py:218
  59.3 0.0 collective-permute-start.3
  59.3 3.8 %shard_map.64 = (bf16[2,2,256,128]{3,2,1,0:T(8,128)(2,1)S(1)}, bf16[2,2,256,128]{3,2,1,0:T(8,128)(2,1)S(1)}, bf16[2,2,256,128]{3,2,1,0:T(8,128)(2,1)S(1)}, bf16[2,2,256,128]{3,2,1,0:T(8,128)(2,1)S(1)}) custom-call(f32[16,256]{1,0:T(8,128)S(1)} %reshape.44.refs_0_, bf16[8,2,64,256]{3,2,1,0:T(8,128)(2,1)S(1)} %bitcast.20, ...), custom_call_target="tpu_custom_call" | custom-call | flops 2147483648 | bytes 4194304 | tf_op jit(solution)/shard_map/pallas_call | solution.py:147
  63.1 2.3 %collective-permute-start.2 = (bf16[2,2,256,128]{3,2,1,0:T(8,128)(2,1)S(1)}, bf16[2,2,256,128]{3,2,1,0:T(8,128)(2,1)S(1)}, u32[]{:S(2)}, u32[]{:S(2)}) collective-permute-start(bf16[2,2,256,128]{3,2,1,0:T(8,128)(2,1)S(1)} %get-tuple-element.17), channel_id=1, source_target_pairs={{0,16},{1,17},{2,18},{3,19},{4,20},{5,21},{6,22},{7,23},{8,24},{9,... | collective-permute-start | bytes 786440 | tf_op jit(solution)/shard_map/ppermute | solution.py:218
  65.4 22.2 %collective-permute-done.5.theirs_ref = bf16[2,2,256,128]{3,2,1,0:T(8,128)(2,1)S(1)} collective-permute-done((bf16[2,2,256,128]{3,2,1,0:T(8,128)(2,1)S(1)}, bf16[2,2,256,128]{3,2,1,0:T(8,128)(2,1)S(1)}, u32[]{:S(2)}, u32[]{:S(2)}) %collective-permute-start.5) | collective-permute-done | bytes 262176 | tf_op jit(solution)/shard_map/ppermute | solution.py:218
  87.7 0.4 trace.4.before_ref
  88.1 5.2 %collective-permute-done.4.theirs_ref = bf16[2,2,256,128]{3,2,1,0:T(8,128)(2,1)S(1)} collective-permute-done((bf16[2,2,256,128]{3,2,1,0:T(8,128)(2,1)S(1)}, bf16[2,2,256,128]{3,2,1,0:T(8,128)(2,1)S(1)}, u32[]{:S(2)}, u32[]{:S(2)}) %collective-permute-start.4) | collective-permute-done | bytes 262176 | tf_op jit(solution)/shard_map/ppermute | solution.py:218
  93.3 0.4 trace.5.before_ref
  93.7 5.2 %collective-permute-done.3.theirs_ref = bf16[2,2,256,128]{3,2,1,0:T(8,128)(2,1)S(1)} collective-permute-done((bf16[2,2,256,128]{3,2,1,0:T(8,128)(2,1)S(1)}, bf16[2,2,256,128]{3,2,1,0:T(8,128)(2,1)S(1)}, u32[]{:S(2)}, u32[]{:S(2)}) %collective-permute-start.3) | collective-permute-done | bytes 262176 | tf_op jit(solution)/shard_map/ppermute | solution.py:218
  98.9 0.4 trace.6.before_ref
  99.3 5.2 %collective-permute-done.2.theirs_ref = bf16[2,2,256,128]{3,2,1,0:T(8,128)(2,1)S(1)} collective-permute-done((bf16[2,2,256,128]{3,2,1,0:T(8,128)(2,1)S(1)}, bf16[2,2,256,128]{3,2,1,0:T(8,128)(2,1)S(1)}, u32[]{:S(2)}, u32[]{:S(2)}) %collective-permute-start.2) | collective-permute-done | bytes 262176 | tf_op jit(solution)/shard_map/ppermute | solution.py:218
  104.5 0.4 trace.7
  104.9 0.1 collective-permute-start.6
  105.0 0.6 collective-permute-start.7
  105.6 2.8 %collective-permute-done.6 = f32[1,2]{1,0:T(1,128)S(1)} collective-permute-done((f32[1,2]{1,0:T(1,128)S(1)}, f32[1,2]{1,0:T(1,128)S(1)}, u32[]{:S(2)}, u32[]{:S(2)}) %collective-permute-start.6) | collective-permute-done | bytes 40 | tf_op jit(solution)/shard_map/ppermute | solution.py:218
  108.3 1.6 %collective-permute-start.8 = (f32[1,2]{1,0:T(1,128)S(1)}, f32[1,2]{1,0:T(1,128)S(1)}, u32[]{:S(2)}, u32[]{:S(2)}) collective-permute-start(f32[1,2]{1,0:T(1,128)S(1)} %collective-permute-done.6), channel_id=1, source_target_pairs={{0,1},{1,0},{2,3},{3,2},{4,5},{5,4},{6,7},{7,6},{8,9},{9,8},{10,11... | collective-permute-start | bytes 32 | tf_op jit(solution)/shard_map/ppermute | solution.py:221
  110.0 0.0 collective-permute-done.7
  110.0 0.8 collective-permute-done.8
  110.8 0.5 add_add_fusion
  (4 shorter events, 0.0 us)
Async XLA Ops:
  0.0 42.6 %copy-start = (s32[16,24]{1,0:T(8,128)S(1)}, s32[16,24]{1,0:T(8,128)}, u32[]{:S(2)}) copy-start(s32[16,24]{1,0:T(8,128)} %param.9) | copy-start | bytes 4612
  4.2 7.7 %copy-start.2 = (s32[16]{0:T(128)S(1)}, s32[16]{0:T(128)}, u32[]{:S(2)}) copy-start(s32[16]{0:T(128)} %param.11) | copy-start | bytes 196
  4.2 48.1 %collective-permute-start.1 = (bf16[4,2,1024,128]{3,2,1,0:T(8,128)(2,1)}, bf16[4,2,1024,128]{3,2,1,0:T(8,128)(2,1)}, u32[]{:S(2)}, u32[]{:S(2)}) collective-permute-start(bf16[4,2,1024,128]{3,2,1,0:T(8,128)(2,1)} %sort.1.refs_2_), channel_id=1, source_target_pairs={{0,1},{1,0},{2,3},{3,2},{4,5},{5,4},{6,7},{7,6},{8,9},{9,8},{10,11... | collective-permute-start | bytes 6291464 | tf_op jit(solution)/shard_map/ppermute | solution.py:221
  7.3 30.1 %all-to-all-start.1 = ((bf16[8,8,2,2048]{3,2,1,0:T(2,128)(2,1)}), bf16[8,8,2,2048]{3,2,1,0:T(2,128)(2,1)S(1)}, u32[]{:S(2)}, u32[]{:S(2)}) async-start(bf16[8,8,2,2048]{3,2,1,0:T(2,128)(2,1)} %get-tuple-element.18), calls=%async_computation.1 | async-start | bytes 1048576 | tf_op jit(solution)/shard_map/all_to_all | solution.py:225
  11.9 25.5 %collective-permute-start = (bf16[8,8,2,2048]{3,2,1,0:T(2,128)(2,1)}, bf16[8,8,2,2048]{3,2,1,0:T(2,128)(2,1)}, u32[]{:S(2)}, u32[]{:S(2)}) collective-permute-start(bf16[8,8,2,2048]{3,2,1,0:T(2,128)(2,1)} %get-tuple-element.15), channel_id=1, source_target_pairs={{0,16},{1,17},{2,18},{3,19},{4,20},{5,21},{6,22},{7,23},{8,24},{9,... | collective-permute-start | bytes 1572872 | tf_op jit(solution)/shard_map/ppermute | solution.py:218
  37.4 12.7 %all-to-all-start = ((bf16[8,8,2,2048]{3,2,1,0:T(2,128)(2,1)}), bf16[8,8,2,2048]{3,2,1,0:T(2,128)(2,1)S(1)}, u32[]{:S(2)}, u32[]{:S(2)}) async-start(bf16[8,8,2,2048]{3,2,1,0:T(2,128)(2,1)} %collective-permute-done), calls=%async_computation | async-start | bytes 1048576 | tf_op jit(solution)/shard_map/all_to_all | solution.py:225
  43.9 8.4 %copy-start.1 = (bf16[4,2,1024,128]{3,2,1,0:T(8,128)(2,1)S(1)}, bf16[4,2,1024,128]{3,2,1,0:T(8,128)(2,1)}, u32[]{:S(2)}) copy-start(bf16[4,2,1024,128]{3,2,1,0:T(8,128)(2,1)} %sort.1.refs_2_) | copy-start | bytes 6291460
  56.2 31.5 %collective-permute-start.5 = (bf16[2,2,256,128]{3,2,1,0:T(8,128)(2,1)S(1)}, bf16[2,2,256,128]{3,2,1,0:T(8,128)(2,1)S(1)}, u32[]{:S(2)}, u32[]{:S(2)}) collective-permute-start(bf16[2,2,256,128]{3,2,1,0:T(8,128)(2,1)S(1)} %get-tuple-element.24), channel_id=1, source_target_pairs={{0,16},{1,17},{2,18},{3,19},{4,20},{5,21},{6,22},{7,23},{8,24},{9,... | collective-permute-start | bytes 786440 | tf_op jit(solution)/shard_map/ppermute | solution.py:218
  56.3 37.0 %collective-permute-start.4 = (bf16[2,2,256,128]{3,2,1,0:T(8,128)(2,1)S(1)}, bf16[2,2,256,128]{3,2,1,0:T(8,128)(2,1)S(1)}, u32[]{:S(2)}, u32[]{:S(2)}) collective-permute-start(bf16[2,2,256,128]{3,2,1,0:T(8,128)(2,1)S(1)} %get-tuple-element.22), channel_id=1, source_target_pairs={{0,17},{1,16},{2,19},{3,18},{4,21},{5,20},{6,23},{7,22},{8,25},{9,... | collective-permute-start | bytes 786440 | tf_op jit(solution)/shard_map/ppermute | solution.py:218
  59.3 39.6 %collective-permute-start.3 = (bf16[2,2,256,128]{3,2,1,0:T(8,128)(2,1)S(1)}, bf16[2,2,256,128]{3,2,1,0:T(8,128)(2,1)S(1)}, u32[]{:S(2)}, u32[]{:S(2)}) collective-permute-start(bf16[2,2,256,128]{3,2,1,0:T(8,128)(2,1)S(1)} %get-tuple-element.20), channel_id=1, source_target_pairs={{0,16},{1,17},{2,18},{3,19},{4,20},{5,21},{6,22},{7,23},{8,24},{9,... | collective-permute-start | bytes 786440 | tf_op jit(solution)/shard_map/ppermute | solution.py:218
  63.1 41.4 %collective-permute-start.2 = (bf16[2,2,256,128]{3,2,1,0:T(8,128)(2,1)S(1)}, bf16[2,2,256,128]{3,2,1,0:T(8,128)(2,1)S(1)}, u32[]{:S(2)}, u32[]{:S(2)}) collective-permute-start(bf16[2,2,256,128]{3,2,1,0:T(8,128)(2,1)S(1)} %get-tuple-element.17), channel_id=1, source_target_pairs={{0,16},{1,17},{2,18},{3,19},{4,20},{5,21},{6,22},{7,23},{8,24},{9,... | collective-permute-start | bytes 786440 | tf_op jit(solution)/shard_map/ppermute | solution.py:218
  104.9 3.4 %collective-permute-start.6 = (f32[1,2]{1,0:T(1,128)S(1)}, f32[1,2]{1,0:T(1,128)S(1)}, u32[]{:S(2)}, u32[]{:S(2)}) collective-permute-start(f32[1,2]{1,0:T(1,128)S(1)} %trace.7), channel_id=1, source_target_pairs={{0,16},{1,17},{2,18},{3,19},{4,20},{5,21},{6,22},{7,23},{8,24},{9,... | collective-permute-start | bytes 32 | tf_op jit(solution)/shard_map/ppermute | solution.py:218
  105.0 4.9 %collective-permute-start.7 = (f32[1,2]{1,0:T(1,128)S(1)}, f32[1,2]{1,0:T(1,128)S(1)}, u32[]{:S(2)}, u32[]{:S(2)}) collective-permute-start(f32[1,2]{1,0:T(1,128)S(1)} %trace.7), channel_id=1, source_target_pairs={{0,1},{1,0},{2,3},{3,2},{4,5},{5,4},{6,7},{7,6},{8,9},{9,8},{10,11... | collective-permute-start | bytes 32 | tf_op jit(solution)/shard_map/ppermute | solution.py:221
  108.3 2.5 %collective-permute-start.8 = (f32[1,2]{1,0:T(1,128)S(1)}, f32[1,2]{1,0:T(1,128)S(1)}, u32[]{:S(2)}, u32[]{:S(2)}) collective-permute-start(f32[1,2]{1,0:T(1,128)S(1)} %collective-permute-done.6), channel_id=1, source_target_pairs={{0,1},{1,0},{2,3},{3,2},{4,5},{5,4},{6,7},{7,6},{8,9},{9,8},{10,11... | collective-permute-start | bytes 32 | tf_op jit(solution)/shard_map/ppermute | solution.py:221
